TPU v7x, 256 devices: a whole 4x4x8 slice. The times are simulated.
256 devices in a mesh: len: 4 (over y), energy: 32 (over z, x), mom: 2 (over core).
Axes of the slice: x: 4, y: 4, z: 8, core: 2. Of those that a mesh axis runs over, the one named last changes fastest.
Arguments:
- hamiltonian: float32 [2, 4, 2, 128, 128], P('mom', 'len'), may hold values from -0.5 to 0.5
- sigma_prev: float32 [2, 4, 128, 2, 128, 128], P('mom', 'len', 'energy'), may hold values from -0.25 to 0.25
- coupling: float32 [4, 128, 128], P('len'), may hold values from -1.5 to 1.5
- coupling_pattern: int32 [128, 128], replicated, may hold values 0 or 1
- phonon_shift: int32 [4], replicated, may hold values from 1 to 64
- phonon_weight: float32 [4], replicated, may hold values from 0.5 to 2
Outputs:
- sigma_retarded: float32 [2, 4, 128, 2, 128, 128], P('mom', 'len', 'energy')
- sigma_lesser: float32 [2, 4, 128, 2, 128, 128], P('mom', 'len', 'energy')
All inputs are finite; a program needn't handle non-finite values.
Results may differ from a plain program's by a relative error of at most 0.0001.
Values sent between devices are 32-bit elements; how exact they have to be, the bound alone decides.
A program may use at most 128 MiB of HBM per device.

v0:
```python
import jax
import jax.numpy as jnp
from jax import lax
from jax.sharding import PartitionSpec as P

NEWTON = 2


HIGHEST = lax.Precision.HIGHEST


def from_behind(array, axis, by):
    size = lax.axis_size(axis)
    pairs = [(i, i + by) for i in range(size) if 0 <= i + by < size]
    return lax.ppermute(array, axis, pairs)


def extended(block, sides, width):
    for axis, dim in sides:
        count = lax.axis_size(axis)
        forward = [(i, i + 1) for i in range(count - 1)]
        backward = [(target, source) for source, target in forward]
        low = lax.ppermute(
            lax.slice_in_dim(block, block.shape[dim] - width, None, axis=dim), axis, forward
        )
        high = lax.ppermute(lax.slice_in_dim(block, 0, width, axis=dim), axis, backward)
        block = jnp.concatenate([low, block, high], axis=dim)
    return block


def partner(value, axis, bit):
    mask = 2**bit
    pairs = [(source, source ^ mask) for source in range(lax.axis_size(axis))]
    return lax.ppermute(value, axis, pairs)


def cmul(left, right):

    def prod(a, b):
        return jnp.einsum("eij,ejk->eik", a, b, precision=HIGHEST)

    real = prod(left[:, 0], right[:, 0]) - prod(left[:, 1], right[:, 1])
    imag = prod(left[:, 0], right[:, 1]) + prod(left[:, 1], right[:, 0])
    return jnp.stack([real, imag], axis=1)


def bond_left(bond, mat):
    return jnp.einsum("ij,ecjk->ecik", bond, mat, precision=HIGHEST)


def bond_right(mat, bond):
    return jnp.einsum("ecij,jk->ecik", mat, bond, precision=HIGHEST)


def scale_by(mat, qre, qim):
    qre = qre[:, None, None]
    qim = qim[:, None, None]
    real = qre * mat[:, 0] - qim * mat[:, 1]
    imag = qre * mat[:, 1] + qim * mat[:, 0]
    return jnp.stack([real, imag], axis=1)


def invert(ham, sig, zre, zim):
    eye = jnp.eye(ham.shape[-1], dtype=jnp.float32)
    eye_c = jnp.stack([eye, jnp.zeros_like(eye)])
    dmat = scale_by(jnp.broadcast_to(eye_c, sig.shape), zre, zim) - ham[None] - sig
    mag = zre * zre + zim * zim
    qre = zre / mag
    qim = -zim / mag
    inverse = scale_by(2.0 * eye_c - scale_by(dmat, qre, qim), qre, qim)
    for step in range(NEWTON):
        inverse = cmul(inverse, 2.0 * eye_c - cmul(dmat, inverse))
    return inverse


def kernels(shift, weight, total):
    index = jnp.arange(total, dtype=jnp.int32)
    own = (index[None, None, :] == index[None, :, None] - shift[:, None, None]).astype(jnp.float32)
    other = (index[None, None, :] == index[None, :, None] + shift[:, None, None]).astype(
        jnp.float32
    )
    own = jnp.sum(weight[:, None, None] * own, axis=0)
    other = jnp.sum(weight[:, None, None] * other, axis=0)
    return (own, other)


def channels(green, occupation):
    diff_re = green[:, 0] - jnp.swapaxes(green[:, 0], -1, -2)
    diff_im = green[:, 1] + jnp.swapaxes(green[:, 1], -1, -2)
    scale = occupation[:, None, None]
    return jnp.stack([green[:, 0], green[:, 1], scale * diff_re, scale * diff_im], axis=1)


def shards(hamiltonian, sigma_prev, coupling, coupling_pattern, phonon_shift, phonon_weight):
    local_e = sigma_prev.shape[2]
    size = hamiltonian.shape[-1]
    layers = lax.axis_size("len")
    total = local_e * lax.axis_size("energy")
    energy_pos = (lax.axis_index("energy") * local_e + jnp.arange(local_e, dtype=jnp.int32)).astype(
        jnp.float32
    )
    zre = 5.0 + 2.0 * energy_pos / total
    zim = jnp.ones_like(zre)
    occupation = 1.0 / (1.0 + jnp.exp(8.0 * energy_pos / total - 4.0))
    bond = coupling[0] * coupling_pattern.astype(jnp.float32)
    block = invert(hamiltonian[0, 0], sigma_prev[0, 0], zre, zim)
    zero = jnp.zeros_like(block)
    gleft = block
    left = zero
    for step in range(layers - 1):
        below = from_behind(gleft, "len", 1)
        left = bond_right(bond_left(bond, below), bond.T)
        if step < layers - 2:
            gleft = block + cmul(cmul(block, left), block)
    sending = bond_right(bond_left(bond.T, block), bond)
    right = zero
    for step in range(layers - 1):
        right = from_behind(sending, "len", -1)
        if step < layers - 2:
            gright = block + cmul(cmul(block, right), block)
            sending = bond_right(bond_left(bond.T, gright), bond)
    green = block + cmul(cmul(block, left + right), block)
    flat = channels(green, occupation).reshape(local_e, 4, size * size)
    regrouped = lax.all_to_all(flat, "energy", split_axis=2, concat_axis=0, tiled=True)
    rims = extended(regrouped[None], (("len", 0),), 1)
    combined = (regrouped + 0.5 * (rims[0] + rims[2]))[None]
    partner_part = partner(combined, "mom", 0)
    own, other = kernels(phonon_shift, phonon_weight, total)
    mixed = jnp.einsum("ef,lfcx->lecx", own, combined, precision=HIGHEST) + 0.5 * jnp.einsum(
        "ef,lfcx->lecx", other, partner_part, precision=HIGHEST
    )
    back = lax.all_to_all(mixed[0], "energy", split_axis=0, concat_axis=2, tiled=True)
    back = back.reshape(local_e, 4, size, size)
    sigma_retarded = back[:, :2].reshape(1, 1, local_e, 2, size, size)
    lesser_part = back[:, 2:]
    sigma_lesser = lesser_part.reshape(1, 1, local_e, 2, size, size)
    return (sigma_retarded, sigma_lesser)


def solution(mesh):
    in_specs = (
        P("mom", "len", None, None, None),
        P("mom", "len", "energy", None, None, None),
        P("len", None, None),
        P(),
        P(),
        P(),
    )
    out_specs = (
        P("mom", "len", "energy", None, None, None),
        P("mom", "len", "energy", None, None, None),
    )
    return jax.shard_map(shards, mesh=mesh, in_specs=in_specs, out_specs=out_specs, check_vma=False)
```

profile of v0, /device:TPU:2, one launch (start us, length us, event | category | flops | bytes accessed | tf_op | source)
XLA Modules:
  0.0 338.7 jit_solution(4922968732122811070)
XLA Ops:
  0.8 1.1 fusion.15
  9.0 3.5 %collective-permute-start = (f32[4,2,128,128]{3,2,0,1:T(8,128)S(1)}, f32[4,2,128,128]{3,2,0,1:T(8,128)S(1)}, u32[]{:S(2)}, u32[]{:S(2)}) collective-permute-start(f32[4,2,128,128]{3,2,0,1:T(8,128)S(1)} %pad_maximum_fusion.1), channel_id=1, source_target_pairs={{0,64},{64,128},{128,192},{1,65},{65,129},{129,193},{2,66},{66,130... | collective-permute-start | bytes 1572872 | tf_op jit(solution)/shard_map/ppermute | solution.py:15
  14.4 1.0 fusion.66
  15.4 1.5 collective-permute-start.3
  16.9 6.7 %collective-permute-done = f32[4,2,128,128]{3,2,0,1:T(8,128)S(1)} collective-permute-done((f32[4,2,128,128]{3,2,0,1:T(8,128)S(1)}, f32[4,2,128,128]{3,2,0,1:T(8,128)S(1)}, u32[]{:S(2)}, u32[]{:S(2)}) %collective-permute-start) | collective-permute-done | bytes 524320 | tf_op jit(solution)/shard_map/ppermute | solution.py:15
  24.6 1.0 fusion.74
  27.6 3.0 collective-permute-done.3
  33.2 3.9 %collective-permute-start.1 = (f32[4,2,128,128]{3,2,0,1:T(8,128)S(1)}, f32[4,2,128,128]{3,2,0,1:T(8,128)S(1)}, u32[]{:S(2)}, u32[]{:S(2)}) collective-permute-start(f32[4,2,128,128]{3,2,0,1:T(8,128)S(1)} %maximum_add_fusion.1), channel_id=1, source_target_pairs={{0,64},{64,128},{128,192},{1,65},{65,129},{129,193},{2,66},{66,130... | collective-permute-start | bytes 1572872 | tf_op jit(solution)/shard_map/ppermute | solution.py:15
  39.1 7.6 %collective-permute-done.1 = f32[4,2,128,128]{3,2,0,1:T(8,128)S(1)} collective-permute-done((f32[4,2,128,128]{3,2,0,1:T(8,128)S(1)}, f32[4,2,128,128]{3,2,0,1:T(8,128)S(1)}, u32[]{:S(2)}, u32[]{:S(2)}) %collective-permute-start.1) | collective-permute-done | bytes 524320 | tf_op jit(solution)/shard_map/ppermute | solution.py:15
  47.7 1.0 fusion.71
  53.0 1.0 fusion.63
  54.0 1.3 collective-permute-start.4
  55.3 5.2 %collective-permute-start.2 = (f32[4,2,128,128]{3,2,0,1:T(8,128)S(1)}, f32[4,2,128,128]{3,2,0,1:T(8,128)S(1)}, u32[]{:S(2)}, u32[]{:S(2)}) collective-permute-start(f32[4,2,128,128]{3,2,0,1:T(8,128)S(1)} %get-tuple-element.14), channel_id=1, source_target_pairs={{0,64},{64,128},{128,192},{1,65},{65,129},{129,193},{2,66},{66,130... | collective-permute-start | bytes 1572872 | tf_op jit(solution)/shard_map/ppermute | solution.py:15
  60.6 7.8 %collective-permute-done.4 = f32[4,2,128,128]{3,2,1,0:T(8,128)S(1)} collective-permute-done((f32[4,2,128,128]{3,2,1,0:T(8,128)S(1)}, f32[4,2,128,128]{3,2,1,0:T(8,128)S(1)}, u32[]{:S(2)}, u32[]{:S(2)}) %collective-permute-start.4) | collective-permute-done | bytes 524320 | tf_op jit(solution)/shard_map/ppermute | solution.py:15
  71.6 1.0 convolution_bitcast_fusion
  72.6 1.8 fusion.60
  74.4 1.3 collective-permute-start.5
  76.9 10.7 %collective-permute-done.5 = f32[4,2,128,128]{3,2,1,0:T(8,128)S(1)} collective-permute-done((f32[4,2,128,128]{3,2,1,0:T(8,128)}, f32[4,2,128,128]{3,2,1,0:T(8,128)S(1)}, u32[]{:S(2)}, u32[]{:S(2)}) %collective-permute-start.5) | collective-permute-done | bytes 524320 | tf_op jit(solution)/shard_map/ppermute | solution.py:15
  87.6 1.0 convolution_add_fusion.1
  93.3 20.4 %copy.149 = f32[4,4,16384]{1,0,2:T(4,128)} copy(f32[4,4,16384]{2,0,1:T(4,128)S(1)} %pad_maximum_fusion) | data formatting | bytes 2097152 | tf_op jit(solution)/shard_map/stack | solution.py:91
  113.7 40.5 %reshape.143 = f32[32,1,8192]{2,1,0:T(1,128)S(1)} reshape(f32[16384,4,4]{2,1,0:T(4,128)} %bitcast.300) | data formatting | bytes 2097152
  154.2 36.3 %all_to_all.33 = f32[32,1,8192]{2,1,0:T(1,128)S(1)} all-to-all(f32[32,1,8192]{2,1,0:T(1,128)S(1)} %reshape.143), channel_id=1, replica_groups=mesh['len'=4,'energy'=32,'mom'=2] {'energy'}, dimensions={0} | all-to-all | bytes 2097152 | tf_op jit(solution)/shard_map/all_to_all | solution.py:124
  191.0 3.2 reduce
  194.2 56.2 %reshape.144 = f32[16384,4,4]{2,1,0:T(4,128)} reshape(f32[32,8192]{1,0:T(8,128)S(1)} %reduce) | data formatting | bytes 2097152
  250.4 19.5 %copy.176 = f32[4,4,32,512]{3,2,1,0:T(8,128)S(1)} copy(f32[4,4,32,512]{1,0,3,2:T(4,128)} %bitcast.301) | data formatting | bytes 2097152 | tf_op jit(solution)/shard_map/all_to_all | solution.py:124
  271.0 3.1 collective-permute-start.6
  274.1 1.3 collective-permute-start.7
  275.4 15.5 %collective-permute-done.6 = f32[1,128,4,512]{1,3,2,0:T(8,128)S(1)} collective-permute-done((f32[1,128,4,512]{1,3,2,0:T(8,128)S(1)}, f32[1,128,4,512]{1,3,2,0:T(8,128)S(1)}, u32[]{:S(2)}, u32[]{:S(2)}) %collective-permute-start.6) | collective-permute-done | bytes 1048608 | tf_op jit(solution)/shard_map/ppermute | solution.py:23
  291.0 4.2 %collective-permute-done.7 = f32[1,128,4,512]{1,3,2,0:T(8,128)S(1)} collective-permute-done((f32[1,128,4,512]{1,3,2,0:T(8,128)S(1)}, f32[1,128,4,512]{1,3,2,0:T(8,128)S(1)}, u32[]{:S(2)}, u32[]{:S(2)}) %collective-permute-start.7) | collective-permute-done | bytes 1048608 | tf_op jit(solution)/shard_map/ppermute | solution.py:26
  296.0 2.3 collective-permute-done.8
  300.9 35.6 %all_to_all.34 = f32[128,4,512]{2,1,0:T(4,128)S(1)} all-to-all(f32[128,4,512]{2,1,0:T(4,128)S(1)} %copy.155), channel_id=1, replica_groups=mesh['len'=4,'energy'=32,'mom'=2] {'energy'}, dimensions={0} | all-to-all | bytes 2097152 | tf_op jit(solution)/shard_map/all_to_all | solution.py:132
  337.2 1.0 slice_bitcast_fusion
  (107 shorter events, 36.1 us)
Async XLA Ops:
  9.0 14.7 %collective-permute-start = (f32[4,2,128,128]{3,2,0,1:T(8,128)S(1)}, f32[4,2,128,128]{3,2,0,1:T(8,128)S(1)}, u32[]{:S(2)}, u32[]{:S(2)}) collective-permute-start(f32[4,2,128,128]{3,2,0,1:T(8,128)S(1)} %pad_maximum_fusion.1), channel_id=1, source_target_pairs={{0,64},{64,128},{128,192},{1,65},{65,129},{129,193},{2,66},{66,130... | collective-permute-start | bytes 1572872 | tf_op jit(solution)/shard_map/ppermute | solution.py:15
  15.4 15.3 %collective-permute-start.3 = (f32[4,2,128,128]{3,2,1,0:T(8,128)S(1)}, f32[4,2,128,128]{3,2,1,0:T(8,128)S(1)}, u32[]{:S(2)}, u32[]{:S(2)}) collective-permute-start(f32[4,2,128,128]{3,2,1,0:T(8,128)S(1)} %fusion.66), channel_id=1, source_target_pairs={{64,0},{128,64},{192,128},{65,1},{129,65},{193,129},{66,2},{130,66... | collective-permute-start | bytes 1572872 | tf_op jit(solution)/shard_map/ppermute | solution.py:15
  33.2 13.5 %collective-permute-start.1 = (f32[4,2,128,128]{3,2,0,1:T(8,128)S(1)}, f32[4,2,128,128]{3,2,0,1:T(8,128)S(1)}, u32[]{:S(2)}, u32[]{:S(2)}) collective-permute-start(f32[4,2,128,128]{3,2,0,1:T(8,128)S(1)} %maximum_add_fusion.1), channel_id=1, source_target_pairs={{0,64},{64,128},{128,192},{1,65},{65,129},{129,193},{2,66},{66,130... | collective-permute-start | bytes 1572872 | tf_op jit(solution)/shard_map/ppermute | solution.py:15
  54.0 14.3 %collective-permute-start.4 = (f32[4,2,128,128]{3,2,1,0:T(8,128)S(1)}, f32[4,2,128,128]{3,2,1,0:T(8,128)S(1)}, u32[]{:S(2)}, u32[]{:S(2)}) collective-permute-start(f32[4,2,128,128]{3,2,1,0:T(8,128)S(1)} %fusion.63), channel_id=1, source_target_pairs={{64,0},{128,64},{192,128},{65,1},{129,65},{193,129},{66,2},{130,66... | collective-permute-start | bytes 1572872 | tf_op jit(solution)/shard_map/ppermute | solution.py:15
  55.3 20.6 %collective-permute-start.2 = (f32[4,2,128,128]{3,2,0,1:T(8,128)S(1)}, f32[4,2,128,128]{3,2,0,1:T(8,128)S(1)}, u32[]{:S(2)}, u32[]{:S(2)}) collective-permute-start(f32[4,2,128,128]{3,2,0,1:T(8,128)S(1)} %get-tuple-element.14), channel_id=1, source_target_pairs={{0,64},{64,128},{128,192},{1,65},{65,129},{129,193},{2,66},{66,130... | collective-permute-start | bytes 1572872 | tf_op jit(solution)/shard_map/ppermute | solution.py:15
  74.4 13.2 %collective-permute-start.5 = (f32[4,2,128,128]{3,2,1,0:T(8,128)}, f32[4,2,128,128]{3,2,1,0:T(8,128)S(1)}, u32[]{:S(2)}, u32[]{:S(2)}) collective-permute-start(f32[4,2,128,128]{3,2,1,0:T(8,128)} %fusion.60), channel_id=1, source_target_pairs={{64,0},{128,64},{192,128},{65,1},{129,65},{193,129},{66,2},{130,66... | collective-permute-start | bytes 1572872 | tf_op jit(solution)/shard_map/ppermute | solution.py:15
  194.2 101.6 %copy-start.1 = (s32[4]{0:T(128)S(1)}, s32[4]{0:T(128)}, u32[]{:S(2)}) copy-start(s32[4]{0:T(128)} %param.10) | copy-start | bytes 52
  194.2 101.6 %copy-start = (f32[4]{0:T(128)S(1)}, f32[4]{0:T(128)}, u32[]{:S(2)}) copy-start(f32[4]{0:T(128)} %param.11) | copy-start | bytes 52
  271.0 20.0 %collective-permute-start.6 = (f32[1,128,4,512]{1,3,2,0:T(8,128)S(1)}, f32[1,128,4,512]{1,3,2,0:T(8,128)S(1)}, u32[]{:S(2)}, u32[]{:S(2)}) collective-permute-start(f32[1,128,4,512]{1,3,2,0:T(8,128)S(1)} %copy.154), channel_id=1, source_target_pairs={{0,64},{64,128},{128,192},{1,65},{65,129},{129,193},{2,66},{66,130... | collective-permute-start | bytes 3145736 | tf_op jit(solution)/shard_map/ppermute | solution.py:23
  274.1 21.0 %collective-permute-start.7 = (f32[1,128,4,512]{1,3,2,0:T(8,128)S(1)}, f32[1,128,4,512]{1,3,2,0:T(8,128)S(1)}, u32[]{:S(2)}, u32[]{:S(2)}) collective-permute-start(f32[1,128,4,512]{1,3,2,0:T(8,128)S(1)} %copy.154), channel_id=1, source_target_pairs={{64,0},{128,64},{192,128},{65,1},{129,65},{193,129},{66,2},{130,66... | collective-permute-start | bytes 3145736 | tf_op jit(solution)/shard_map/ppermute | solution.py:26
  295.4 3.0 collective-permute-start.8
where the time goes:
time: 345 us; the launch traced here: 339 us
  local copies, waits for them, and re-layouts  141 us (41%)
  blocking collectives  71.9 us (21%)
  waiting for transfers between devices  57.8 us (17%)
  matrix products  37 us (11%)
  starting transfers between devices  21.5 us (6%)
  other arithmetic  7.21 us (2%)
    unnamed x7, local copies, waits for them, and re-layouts  96.8 us
    all_to_all x1, blocking collectives, shards(): lax.all_to_all(flat, 'energy', split_axis=2, concat_axis=0, tiled=True)  36.3 us
    ppermute x6, waiting for transfers between devices, from_behind(): return lax.ppermute(array, axis, pairs)  35.7 us
    all_to_all x1, blocking collectives, shards(): lax.all_to_all(mixed[0], 'energy', split_axis=0, concat_axis=2, tiled=True)  35.6 us
    dot_general x56, matrix products, prod(): return jnp.einsum('eij,ejk->eik', a, b, precision=HIGHEST)  22.3 us
    all_to_all x4, local copies, waits for them, and re-layouts, shards(): lax.all_to_all(flat, 'energy', split_axis=2, concat_axis=0, tiled=True)  21.1 us
    another operation x3, local copies, waits for them, and re-layouts, channels(): jnp.stack([green[:, 0], green[:, 1], scale * diff_re, scale * diff_im], a...  20.6 us
    ppermute x6, starting transfers between devices, from_behind(): return lax.ppermute(array, axis, pairs)  16.7 us
  transfers between devices with their start and end apart: 9, of which 8 were waited for; matrix products, arithmetic and copies ran while one was open for 5% of the time, Pallas kernels for 0%

commit v1 on v0

v1 whole, which is shorter than its diff:
```python
import functools

import jax
import jax.numpy as jnp
from jax import lax
from jax.experimental import pallas as pl
from jax.experimental.pallas import tpu as pltpu
from jax.sharding import PartitionSpec as P

N = 128
LAYERS = 4
ENERGIES = 128
GROUPS = 32
ZS, XS = 8, 4
MOMS = 2
PEERS = GROUPS * MOMS
PHONONS = 4
F32 = jnp.float32
BF16 = jnp.bfloat16
MESH = pl.DeviceIdType.MESH


def wrap(value, size):
    return jnp.where(value >= size, value - size, value)


def device(layer, group, mom):
    return (layer, group, mom)


def split(value):
    high = value.astype(BF16)
    return high, (value - high.astype(F32)).astype(BF16)


def lhs3(parts, axis=1):
    high = jnp.concatenate([p[0] for p in parts], axis=axis)
    low = jnp.concatenate([p[1] for p in parts], axis=axis)
    return jnp.concatenate([high, high, low], axis=1)


def dot(left, right):
    return jnp.dot(left, right, preferred_element_type=F32)


def left_c(re, im):
    return lhs3([split(re), split(im)])


def right_c(re, im):
    rh, rl = split(re)
    ih, il = split(im)
    high = jnp.concatenate(
        [jnp.concatenate([rh, ih], axis=1), jnp.concatenate([-ih, rh], axis=1)], axis=0
    )
    low = jnp.concatenate(
        [jnp.concatenate([rl, il], axis=1), jnp.concatenate([-il, rl], axis=1)], axis=0
    )
    return jnp.concatenate([high, low, high], axis=0)


def cmul(left, right):
    both = dot(left, right)
    return both[:, :N], both[:, N:]


def right_plain(parts):
    high = jnp.concatenate([p[0] for p in parts], axis=1)
    low = jnp.concatenate([p[1] for p in parts], axis=1)
    return jnp.concatenate([high, low, high], axis=0)


def sandwich(first, re, im, second):
    both = dot(first, right_plain([split(re), split(im)]))
    stacked = jnp.concatenate([both[:, :N], both[:, N:]], axis=0)
    out = dot(lhs3([split(stacked)]), second)
    return out[:N], out[N:]


def main_kernel(
    ham, sig, coup, pat, shift, weight, back,
    gout, blocks, bonds, greens, send, recv, mixed,
    swap_send, swap_recv, bond_send, bond_recv,
    fwd_send, fwd_recv, ret_send, ret_recv,
):
    l = lax.axis_index("len")
    group = lax.axis_index("energy")
    k = lax.axis_index("mom")
    z = group // XS
    x = group - z * XS
    ls = [wrap(l + i, LAYERS) for i in range(LAYERS)]
    xs = [wrap(x + i, XS) for i in range(XS)]
    ks = [k, 1 - k]

    def plane(body):
        for dx in range(XS):
            for dk in range(MOMS):
                if dx or dk:
                    body(z * XS + xs[dx], ks[dk])

        def step(dz, carry):
            base = wrap(z + dz, ZS) * XS
            for dx in range(XS):
                for dk in range(MOMS):
                    body(base + xs[dx], ks[dk])
            return carry

        lax.fori_loop(1, ZS, step, 0)

    barrier = pltpu.get_barrier_semaphore()

    def greet(layer):
        def body(to_group, to_mom):
            pl.semaphore_signal(
                barrier, inc=1, device_id=device(layer, to_group, to_mom), device_id_type=MESH
            )
        return body

    for i in range(LAYERS):
        plane(greet(ls[i]))
        if i:
            greet(ls[i])(group, k)

    bonds[l] = coup[...] * pat[...].astype(F32)

    def inverse(i):
        e = (group * LAYERS + i).astype(F32)
        zre = 5.0 + 2.0 * e / ENERGIES
        mag = zre * zre + 1.0
        qre = jnp.full((1, 1), zre / mag, F32)
        qim = jnp.full((1, 1), -1.0 / mag, F32)
        sre = ham[0] + sig[i, 0]
        sim = ham[1] + sig[i, 1]
        wre = qre * sre - qim * sim
        wim = qre * sim + qim * sre
        wl = left_c(wre, wim)
        w2re, w2im = cmul(wl, right_c(wre, wim))
        w2r = right_c(w2re, w2im)
        w4re, w4im = cmul(left_c(w2re, w2im), w2r)
        tre, tim = cmul(wl, w2r)
        eye = (
            lax.broadcasted_iota(jnp.int32, (N, N), 0) == lax.broadcasted_iota(jnp.int32, (N, N), 1)
        ).astype(F32)
        are = eye + wre + w2re + tre
        aim = wim + w2im + tim
        bre, bim = cmul(left_c(are, aim), right_c(w4re, w4im))
        are = are + bre
        aim = aim + bim
        return qre * are - qim * aim, qre * aim + qim * are

    def swap(i):
        return pltpu.make_async_remote_copy(
            src_ref=gout.at[i], dst_ref=blocks.at[l], send_sem=swap_send, recv_sem=swap_recv,
            device_id=device(i, group, k), device_id_type=MESH,
        )

    def bond_copy(i):
        return pltpu.make_async_remote_copy(
            src_ref=bonds.at[l], dst_ref=bonds.at[l], send_sem=bond_send, recv_sem=bond_recv,
            device_id=device(i, group, k), device_id_type=MESH,
        )

    for pair in ((2, 1), (3, 0)):
        done = [inverse(ls[d]) for d in pair]
        for d, (re, im) in zip(pair, done):
            if d:
                gout[ls[d], 0] = re
                gout[ls[d], 1] = im
            else:
                blocks[l, 0] = re
                blocks[l, 1] = im
        if pair[0] == 2:
            pl.semaphore_wait(barrier, LAYERS * PEERS - 1)
        for d in pair:
            if d:
                swap(ls[d]).start()
                bond_copy(ls[d]).start()

    three = blocks.at[pl.ds(0, LAYERS - 1)]
    pltpu.make_async_copy(three, three, swap_recv).wait()
    bthree = bonds.at[pl.ds(0, LAYERS - 1)]
    pltpu.make_async_copy(bthree, bthree, bond_recv).wait()

    g = [(blocks[i, 0], blocks[i, 1]) for i in range(LAYERS)]
    gl3 = [left_c(*b) for b in g]
    gr3 = [right_c(*b) for b in g]
    b_l, b_r, bt_l, bt_r = {}, {}, {}, {}
    for i in range(1, LAYERS):
        b = bonds[i]
        bs, bts = split(b), split(b.T)
        b_l[i], bt_l[i] = lhs3([bs]), lhs3([bts])
        b_r[i], bt_r[i] = right_plain([bs]), right_plain([bts])

    def dress(i, term):
        tre, tim = cmul(gl3[i], right_c(*term))
        sre, sim = cmul(left_c(tre, tim), gr3[i])
        return g[i][0] + sre, g[i][1] + sim

    down = {0: g[0]}
    up = {LAYERS - 1: g[LAYERS - 1]}
    for step in range(1, LAYERS):
        i = step
        down[i] = dress(i, sandwich(b_l[i], *down[i - 1], bt_r[i]))
        j = LAYERS - 1 - step
        up[j] = dress(j, sandwich(bt_l[j + 1], *up[j + 1], b_r[j + 1]))
    for c in range(2):
        zero = jnp.zeros((N, N), F32)
        greens[0, c] = zero
        greens[LAYERS + 1, c] = zero
        for i in range(LAYERS):
            greens[i + 1, c] = down[i][c] + (up[i][c] - g[i][c])

    rows = lax.broadcasted_iota(jnp.int32, (N, N), 0)
    cols = lax.broadcasted_iota(jnp.int32, (N, N), 1)
    upper = rows < cols
    slot = group * LAYERS + l

    for t in range(LAYERS):
        layer = ls[t]
        yre = greens[layer + 1, 0] + 0.5 * (greens[layer, 0] + greens[layer + 2, 0])
        yim = greens[layer + 1, 1] + 0.5 * (greens[layer, 1] + greens[layer + 2, 1])
        tre, tim = yre.T, yim.T
        pmat = jnp.where(upper, yre - tre, yim + tim)
        qmat = jnp.where(upper, yim - tim, yre + tre)
        send[layer, :, 0, :] = pmat[: N // 2]
        send[layer, :, 1, :] = pmat[N // 2 :]
        send[layer, :, 2, :] = qmat[: N // 2]
        send[layer, :, 3, :] = qmat[N // 2 :]

        def forward(to_group, to_mom, layer=layer):
            pltpu.make_async_remote_copy(
                src_ref=send.at[layer, to_group * MOMS + to_mom], dst_ref=recv.at[k, slot],
                send_sem=fwd_send, recv_sem=fwd_recv,
                device_id=device(layer, to_group, to_mom), device_id_type=MESH,
            ).start()

        plane(forward)
        if t:
            forward(group, k)
        else:
            pltpu.make_async_copy(
                send.at[layer, group * MOMS + k], recv.at[k, slot], fwd_recv
            ).start()

    dist = rows - cols
    own = jnp.zeros((N, N), F32)
    other = jnp.zeros((N, N), F32)
    for m in range(PHONONS):
        own = own + jnp.where(dist == shift[m], weight[m], 0.0)
        other = other + jnp.where(dist == -shift[m], weight[m], 0.0)
    other = 0.5 * other
    occupation = 1.0 / (1.0 + jnp.exp(8.0 * cols.astype(F32) / ENERGIES - 4.0))
    ret_w = jnp.concatenate(
        [jnp.concatenate([own, other], axis=1), jnp.concatenate([other, own], axis=1)], axis=0
    )
    fown, fother = own * occupation, other * occupation
    les_w = jnp.concatenate(
        [jnp.concatenate([fown, fother], axis=1), jnp.concatenate([fother, fown], axis=1)], axis=0
    )
    ret_l, les_l = lhs3([split(ret_w)]), lhs3([split(les_w)])

    pltpu.make_async_copy(recv, recv, fwd_recv).wait()
    pieces = []
    for r in range(4):
        pieces.append(split(jnp.concatenate([recv[0, :, r, :], recv[1, :, r, :]], axis=0)))
    ret = dot(ret_l, right_plain(pieces))
    les = dot(les_l, right_plain(pieces[:2]))
    for c in range(MOMS):
        for r in range(6):
            src = ret if r < 4 else les
            lane = (r if r < 4 else r - 4) * N
            mixed[c, pl.ds(r, N, stride=6), :] = src[c * N : (c + 1) * N, lane : lane + N]

    spot = group * MOMS + k

    def returning(to_group, to_mom):
        pltpu.make_async_remote_copy(
            src_ref=mixed.at[to_mom, pl.ds(pl.multiple_of(to_group * 24, 8), 24), :],
            dst_ref=back.at[spot], send_sem=ret_send, recv_sem=ret_recv,
            device_id=device(l, to_group, to_mom), device_id_type=MESH,
        ).start()

    plane(returning)
    pltpu.make_async_copy(
        mixed.at[k, pl.ds(pl.multiple_of(group * 24, 8), 24), :], back.at[spot], ret_recv
    ).start()

    whole = back.at[pl.ds(0, PEERS)]
    pltpu.make_async_copy(whole, whole, ret_recv).wait()
    sent = back.at[pl.ds(0, PEERS - 1)]
    pltpu.make_async_copy(sent, sent, ret_send).wait()
    pltpu.make_async_copy(three, three, swap_send).wait()
    pltpu.make_async_copy(bthree, bthree, bond_send).wait()
    for i in range(LAYERS):
        part = send.at[i] if i else send.at[0, pl.ds(0, PEERS - 1)]
        pltpu.make_async_copy(part, part, fwd_send).wait()


def unpack_kernel(back, ret, les):
    e = pl.program_id(0)
    rows = lax.broadcasted_iota(jnp.int32, (N, N), 0)
    cols = lax.broadcasted_iota(jnp.int32, (N, N), 1)
    upper = rows < cols

    def whole(r):
        return jnp.concatenate(
            [back[pl.ds(6 * e + r + h, PEERS, stride=24), :] for h in range(2)], axis=0
        )

    pmat, qmat, lmat = whole(0), whole(2), whole(4)
    pt, qt, lt = pmat.T, qmat.T, lmat.T
    off = rows != cols
    zero = jnp.zeros((N, N), F32)
    ret[0, 0, 0, 0] = 0.5 * jnp.where(upper, pmat + qt, qmat - jnp.where(off, pt, zero))
    ret[0, 0, 0, 1] = 0.5 * jnp.where(upper, pt + qmat, pmat - jnp.where(off, qt, zero))
    les[0, 0, 0, 0] = jnp.where(upper, lmat, jnp.where(off, -lt, zero))
    les[0, 0, 0, 1] = jnp.where(upper, lt, lmat)


def shards(hamiltonian, sigma_prev, coupling, coupling_pattern, phonon_shift, phonon_weight):
    vmem = pl.BlockSpec(memory_space=pltpu.VMEM)
    smem = pl.BlockSpec(memory_space=pltpu.SMEM)
    dma = pltpu.SemaphoreType.DMA
    back = pl.pallas_call(
        main_kernel,
        out_shape=jax.ShapeDtypeStruct((PEERS + 1, 24, N), F32),
        in_specs=[vmem] * 4 + [smem] * 2,
        out_specs=vmem,
        scratch_shapes=[
            pltpu.VMEM((LAYERS, 2, N, N), F32),
            pltpu.VMEM((LAYERS, 2, N, N), F32),
            pltpu.VMEM((LAYERS, N, N), F32),
            pltpu.VMEM((LAYERS + 2, 2, N, N), F32),
            pltpu.VMEM((LAYERS, PEERS, 4, N), F32),
            pltpu.VMEM((MOMS, ENERGIES, 4, N), F32),
            pltpu.VMEM((MOMS, 6 * ENERGIES + 8, N), F32),
        ]
        + [dma] * 8,
        compiler_params=pltpu.CompilerParams(collective_id=0, has_side_effects=True),
        name="selfenergy",
    )(
        hamiltonian[0, 0], sigma_prev[0, 0], coupling[0], coupling_pattern,
        phonon_shift, phonon_weight,
    )
    shape = jax.ShapeDtypeStruct((1, 1, 4, 2, N, N), F32)
    out_spec = pl.BlockSpec((1, 1, 1, 2, N, N), lambda e: (0, 0, e, 0, 0, 0))
    return pl.pallas_call(
        unpack_kernel,
        grid=(4,),
        out_shape=(shape, shape),
        in_specs=[pl.BlockSpec(((PEERS + 1) * 24, N), lambda e: (0, 0))],
        out_specs=(out_spec, out_spec),
        name="unpack",
    )(back.reshape((PEERS + 1) * 24, N))


def solution(mesh):
    in_specs = (
        P("mom", "len", None, None, None),
        P("mom", "len", "energy", None, None, None),
        P("len", None, None),
        P(),
        P(),
        P(),
    )
    out_specs = (
        P("mom", "len", "energy", None, None, None),
        P("mom", "len", "energy", None, None, None),
    )
    return jax.shard_map(shards, mesh=mesh, in_specs=in_specs, out_specs=out_specs, check_vma=False)
```

time: 345 us -> 72.2 us (0.21)
  the two profiles are of different devices: /device:TPU:2 before, /device:TPU:1 now
where the time goes in v1:
time: 72.2 us; the launch traced here: 72.1 us
  Pallas kernels  71.4 us (99%)
    pallas_call x1, Pallas kernels, shards(): pl.pallas_call(main_kernel, out_shape=jax.ShapeDtypeStruct((PEERS + 1, 24...  68.5 us
    pallas_call x1, Pallas kernels, shards(): pl.pallas_call(unpack_kernel, grid=(4,), out_shape=(shape, shape), in_spe...  2.92 us

profile of v1, /device:TPU:1, one launch (start us, length us, event | category | flops | bytes accessed | tf_op | source)
XLA Modules:
  0.0 72.1 jit_solution(10187945275676373495)
XLA Ops:
  0.6 68.5 %selfenergy.1 = f32[65,24,128]{2,1,0:T(8,128)} custom-call(f32[2,128,128]{2,1,0:T(8,128)} %bitcast.6, f32[4,2,128,128]{3,2,1,0:T(8,128)} %bitcast.5, f32[128,128]{1,0:T(8,128)} %bitcast.7, s32[128,128]{1,0:T(8,128)} %pat.1, s32[4]{0:T(128)} %shift.1, f32[4]{0:T(128)} %weight.1), custom_call_target="tpu_custom_call" | custom-call | tf_op jit(solution)/shard_map/selfenergy/pallas_call | solution.py:324
  69.1 2.9 %unpack.1 = (f32[1,1,4,2,128,128]{5,4,3,2,1,0:T(8,128)}, f32[1,1,4,2,128,128]{5,4,3,2,1,0:T(8,128)}) custom-call(f32[1560,128]{1,0:T(8,128)} %bitcast.4), custom_call_target="tpu_custom_call" | custom-call | tf_op jit(solution)/shard_map/unpack/pallas_call | solution.py:347

commit v2 on v1

--- a/solution.py
+++ b/solution.py
@@ -81,7 +81,7 @@
     ham, sig, coup, pat, shift, weight, back,
     gout, blocks, bonds, greens, send, recv, mixed,
     swap_send, swap_recv, bond_send, bond_recv,
-    fwd_send, fwd_recv, ret_send, ret_recv,
+    fwd_send, fwd_recv, ret_send, ret_recv, x_sem, z_sem, y_sem,
 ):
     l = lax.axis_index("len")
     group = lax.axis_index("energy")
@@ -107,19 +107,15 @@
 
         lax.fori_loop(1, ZS, step, 0)
 
+    def tell(semaphore, targets):
+        for target in targets:
+            pl.semaphore_signal(semaphore, inc=1, device_id=target, device_id_type=MESH)
+
+    x_line = [device(l, z * XS + xs[i], k) for i in range(1, XS)]
+    z_line = [device(l, wrap(z + i, ZS) * XS + x, k) for i in range(1, ZS)]
+    y_line = [device(ls[i], group, k) for i in range(1, LAYERS)]
     barrier = pltpu.get_barrier_semaphore()
-
-    def greet(layer):
-        def body(to_group, to_mom):
-            pl.semaphore_signal(
-                barrier, inc=1, device_id=device(layer, to_group, to_mom), device_id_type=MESH
-            )
-        return body
-
-    for i in range(LAYERS):
-        plane(greet(ls[i]))
-        if i:
-            greet(ls[i])(group, k)
+    tell(barrier, y_line + x_line + z_line + [device(l, group, 1 - k)])
 
     bonds[l] = coup[...] * pat[...].astype(F32)
 
@@ -170,16 +166,22 @@
                 blocks[l, 0] = re
                 blocks[l, 1] = im
         if pair[0] == 2:
-            pl.semaphore_wait(barrier, LAYERS * PEERS - 1)
+            pl.semaphore_wait(barrier, LAYERS + XS + ZS - 2)
+            tell(x_sem, x_line)
         for d in pair:
             if d:
                 swap(ls[d]).start()
                 bond_copy(ls[d]).start()
 
+    pl.semaphore_wait(x_sem, XS - 1)
+    tell(z_sem, z_line)
     three = blocks.at[pl.ds(0, LAYERS - 1)]
     pltpu.make_async_copy(three, three, swap_recv).wait()
     bthree = bonds.at[pl.ds(0, LAYERS - 1)]
     pltpu.make_async_copy(bthree, bthree, bond_recv).wait()
+
+    pl.semaphore_wait(z_sem, ZS - 1)
+    tell(y_sem, y_line)
 
     g = [(blocks[i, 0], blocks[i, 1]) for i in range(LAYERS)]
     gl3 = [left_c(*b) for b in g]
@@ -215,6 +217,7 @@
     upper = rows < cols
     slot = group * LAYERS + l
 
+    pl.semaphore_wait(y_sem, LAYERS - 1)
     for t in range(LAYERS):
         layer = ls[t]
         yre = greens[layer + 1, 0] + 0.5 * (greens[layer, 0] + greens[layer + 2, 0])
@@ -335,7 +338,8 @@
             pltpu.VMEM((MOMS, ENERGIES, 4, N), F32),
             pltpu.VMEM((MOMS, 6 * ENERGIES + 8, N), F32),
         ]
-        + [dma] * 8,
+        + [dma] * 8
+        + [pltpu.SemaphoreType.REGULAR] * 3,
         compiler_params=pltpu.CompilerParams(collective_id=0, has_side_effects=True),
         name="selfenergy",
     )(

time: 72.2 us -> 68.1 us (0.943)
  Pallas kernels: 71.4 us -> 67.3 us
    pallas_call x1, Pallas kernels: 68.5 us -> 64.4 us  [shards(): pl.pallas_call(main_kernel, out_shape=jax.ShapeDtypeStruct((PEERS + 1, 24...]
where the time goes in v2:
time: 68.1 us; the launch traced here: 67.9 us
  Pallas kernels  67.3 us (99%)
    pallas_call x1, Pallas kernels, shards(): pl.pallas_call(main_kernel, out_shape=jax.ShapeDtypeStruct((PEERS + 1, 24...  64.4 us
    pallas_call x1, Pallas kernels, shards(): pl.pallas_call(unpack_kernel, grid=(4,), out_shape=(shape, shape), in_spe...  2.92 us

profile of v2, /device:TPU:1, one launch (start us, length us, event | category | flops | bytes accessed | tf_op | source)
XLA Modules:
  0.0 67.9 jit_solution(14009891469302670444)
XLA Ops:
  0.6 64.4 %selfenergy.1 = f32[65,24,128]{2,1,0:T(8,128)} custom-call(f32[2,128,128]{2,1,0:T(8,128)} %bitcast.6, f32[4,2,128,128]{3,2,1,0:T(8,128)} %bitcast.5, f32[128,128]{1,0:T(8,128)} %bitcast.7, s32[128,128]{1,0:T(8,128)} %pat.1, s32[4]{0:T(128)} %shift.1, f32[4]{0:T(128)} %weight.1), custom_call_target="tpu_custom_call" | custom-call | tf_op jit(solution)/shard_map/selfenergy/pallas_call | solution.py:327
  65.0 2.9 %unpack.1 = (f32[1,1,4,2,128,128]{5,4,3,2,1,0:T(8,128)}, f32[1,1,4,2,128,128]{5,4,3,2,1,0:T(8,128)}) custom-call(f32[1560,128]{1,0:T(8,128)} %bitcast.4), custom_call_target="tpu_custom_call" | custom-call | tf_op jit(solution)/shard_map/unpack/pallas_call | solution.py:351

commit v3 on v2

--- a/solution.py
+++ b/solution.py
@@ -15,6 +15,7 @@
 MOMS = 2
 PEERS = GROUPS * MOMS
 PHONONS = 4
+ORDER = [(dx, dk) for dx in (2, 1, 3, 0) for dk in (1, 0)]
 F32 = jnp.float32
 BF16 = jnp.bfloat16
 MESH = pl.DeviceIdType.MESH
@@ -78,10 +79,12 @@
 
 
 def main_kernel(
-    ham, sig, coup, pat, shift, weight, back,
+    ham_in, sig_in, coup_in, pat_in, shift, weight, back,
+    ham, sig, coup, pat,
     gout, blocks, bonds, greens, send, recv, mixed,
     swap_send, swap_recv, bond_send, bond_recv,
-    fwd_send, fwd_recv, ret_send, ret_recv, x_sem, z_sem, y_sem,
+    fwd_send, fwd_recv, ret_send, ret_recv, in_sems,
+    x_sem, z_sem, y_sem, core_sem,
 ):
     l = lax.axis_index("len")
     group = lax.axis_index("energy")
@@ -93,31 +96,45 @@
     ks = [k, 1 - k]
 
     def plane(body):
-        for dx in range(XS):
-            for dk in range(MOMS):
-                if dx or dk:
-                    body(z * XS + xs[dx], ks[dk])
-
-        def step(dz, carry):
-            base = wrap(z + dz, ZS) * XS
-            for dx in range(XS):
-                for dk in range(MOMS):
-                    body(base + xs[dx], ks[dk])
+        def line(base, skip=0):
+            for dx, dk in ORDER[: XS * MOMS - skip]:
+                body(base + xs[dx], ks[dk])
+
+        line(wrap(z + ZS // 2, ZS) * XS)
+
+        def step(i, carry):
+            ahead = wrap(z + ZS // 2 - i, ZS) * XS
+            behind = wrap(z + ZS // 2 + i, ZS) * XS
+            for dx, dk in ORDER:
+                body(ahead + xs[dx], ks[dk])
+                body(behind + xs[dx], ks[dk])
             return carry
 
-        lax.fori_loop(1, ZS, step, 0)
+        lax.fori_loop(1, ZS // 2, step, 0)
+        line(z * XS, skip=1)
 
     def tell(semaphore, targets):
         for target in targets:
             pl.semaphore_signal(semaphore, inc=1, device_id=target, device_id_type=MESH)
 
     x_line = [device(l, z * XS + xs[i], k) for i in range(1, XS)]
-    z_line = [device(l, wrap(z + i, ZS) * XS + x, k) for i in range(1, ZS)]
+    z_near = [device(l, wrap(z + i, ZS) * XS + x, k) for i in (1, 2, ZS - 2, ZS - 1)]
     y_line = [device(ls[i], group, k) for i in range(1, LAYERS)]
+    other_core = [device(l, group, 1 - k)]
     barrier = pltpu.get_barrier_semaphore()
-    tell(barrier, y_line + x_line + z_line + [device(l, group, 1 - k)])
-
-    bonds[l] = coup[...] * pat[...].astype(F32)
+    tell(barrier, y_line + x_line + z_near + other_core)
+
+    loads = [
+        pltpu.make_async_copy(ham_in, ham, in_sems.at[0]),
+        pltpu.make_async_copy(sig_in.at[ls[2]], sig.at[ls[2]], in_sems.at[1]),
+        pltpu.make_async_copy(sig_in.at[ls[1]], sig.at[ls[1]], in_sems.at[2]),
+        pltpu.make_async_copy(sig_in.at[ls[3]], sig.at[ls[3]], in_sems.at[3]),
+        pltpu.make_async_copy(coup_in, coup, in_sems.at[4]),
+        pltpu.make_async_copy(pat_in, pat, in_sems.at[5]),
+        pltpu.make_async_copy(sig_in.at[l], sig.at[l], in_sems.at[6]),
+    ]
+    for load in loads:
+        load.start()
 
     def inverse(i):
         e = (group * LAYERS + i).astype(F32)
@@ -156,32 +173,43 @@
             device_id=device(i, group, k), device_id_type=MESH,
         )
 
-    for pair in ((2, 1), (3, 0)):
-        done = [inverse(ls[d]) for d in pair]
-        for d, (re, im) in zip(pair, done):
-            if d:
-                gout[ls[d], 0] = re
-                gout[ls[d], 1] = im
-            else:
-                blocks[l, 0] = re
-                blocks[l, 1] = im
-        if pair[0] == 2:
-            pl.semaphore_wait(barrier, LAYERS + XS + ZS - 2)
-            tell(x_sem, x_line)
-        for d in pair:
-            if d:
-                swap(ls[d]).start()
-                bond_copy(ls[d]).start()
-
+    def keep(where, i, block):
+        where[i, 0], where[i, 1] = block
+
+    loads[0].wait()
+    loads[1].wait()
+    keep(gout, ls[2], inverse(ls[2]))
+    pl.semaphore_wait(barrier, LAYERS + XS + 3)
+    tell(z_sem, z_near)
+    swap(ls[2]).start()
+
+    loads[2].wait()
+    loads[3].wait()
+    one, two = inverse(ls[1]), inverse(ls[3])
+    keep(gout, ls[1], one)
+    keep(gout, ls[3], two)
+    swap(ls[1]).start()
+    swap(ls[3]).start()
+    pl.semaphore_wait(z_sem, 4)
+    tell(x_sem, x_line)
+
+    loads[4].wait()
+    loads[5].wait()
+    bonds[l] = coup[...] * pat[...].astype(F32)
+    for i in (2, 1, 3):
+        bond_copy(ls[i]).start()
+    loads[6].wait()
+    keep(blocks, l, inverse(l))
     pl.semaphore_wait(x_sem, XS - 1)
-    tell(z_sem, z_line)
+    tell(y_sem, y_line)
+
     three = blocks.at[pl.ds(0, LAYERS - 1)]
     pltpu.make_async_copy(three, three, swap_recv).wait()
     bthree = bonds.at[pl.ds(0, LAYERS - 1)]
     pltpu.make_async_copy(bthree, bthree, bond_recv).wait()
 
-    pl.semaphore_wait(z_sem, ZS - 1)
-    tell(y_sem, y_line)
+    pl.semaphore_wait(y_sem, LAYERS - 1)
+    tell(core_sem, other_core)
 
     g = [(blocks[i, 0], blocks[i, 1]) for i in range(LAYERS)]
     gl3 = [left_c(*b) for b in g]
@@ -217,8 +245,8 @@
     upper = rows < cols
     slot = group * LAYERS + l
 
-    pl.semaphore_wait(y_sem, LAYERS - 1)
-    for t in range(LAYERS):
+    pl.semaphore_wait(core_sem, 1)
+    for t in (2, 1, 3, 0):
         layer = ls[t]
         yre = greens[layer + 1, 0] + 0.5 * (greens[layer, 0] + greens[layer + 2, 0])
         yim = greens[layer + 1, 1] + 0.5 * (greens[layer, 1] + greens[layer + 2, 1])
@@ -327,9 +355,13 @@
     back = pl.pallas_call(
         main_kernel,
         out_shape=jax.ShapeDtypeStruct((PEERS + 1, 24, N), F32),
-        in_specs=[vmem] * 4 + [smem] * 2,
+        in_specs=[pl.BlockSpec(memory_space=pl.ANY)] * 4 + [smem] * 2,
         out_specs=vmem,
         scratch_shapes=[
+            pltpu.VMEM((2, N, N), F32),
+            pltpu.VMEM((4, 2, N, N), F32),
+            pltpu.VMEM((N, N), F32),
+            pltpu.VMEM((N, N), jnp.int32),
             pltpu.VMEM((LAYERS, 2, N, N), F32),
             pltpu.VMEM((LAYERS, 2, N, N), F32),
             pltpu.VMEM((LAYERS, N, N), F32),
@@ -339,7 +371,8 @@
             pltpu.VMEM((MOMS, 6 * ENERGIES + 8, N), F32),
         ]
         + [dma] * 8
-        + [pltpu.SemaphoreType.REGULAR] * 3,
+        + [dma((7,))]
+        + [pltpu.SemaphoreType.REGULAR] * 4,
         compiler_params=pltpu.CompilerParams(collective_id=0, has_side_effects=True),
         name="selfenergy",
     )(

time: 68.1 us -> 64.5 us (0.947)
  Pallas kernels: 67.3 us -> 63.8 us
    pallas_call x1, Pallas kernels: 64.4 us -> 60.8 us  [shards(): pl.pallas_call(main_kernel, out_shape=jax.ShapeDtypeStruct((PEERS + 1, 24...]
where the time goes in v3:
time: 64.5 us; the launch traced here: 64.4 us
  Pallas kernels  63.8 us (99%)
    pallas_call x1, Pallas kernels, shards(): pl.pallas_call(main_kernel, out_shape=jax.ShapeDtypeStruct((PEERS + 1, 24...  60.8 us
    pallas_call x1, Pallas kernels, shards(): pl.pallas_call(unpack_kernel, grid=(4,), out_shape=(shape, shape), in_spe...  2.92 us

profile of v3, /device:TPU:1, one launch (start us, length us, event | category | flops | bytes accessed | tf_op | source)
XLA Modules:
  0.0 64.4 jit_solution(2415739114047353391)
XLA Ops:
  0.6 60.8 %selfenergy.1 = f32[65,24,128]{2,1,0:T(8,128)} custom-call(f32[2,128,128]{2,1,0:T(8,128)} %bitcast.6, f32[4,2,128,128]{3,2,1,0:T(8,128)} %bitcast.5, f32[128,128]{1,0:T(8,128)} %bitcast.7, s32[128,128]{1,0:T(8,128)} %pat_in.1, s32[4]{0:T(128)} %shift.1, f32[4]{0:T(128)} %weight.1), custom_call_target="tpu_custom_call" | custom-call | tf_op jit(solution)/shard_map/selfenergy/pallas_call | solution.py:355
  61.5 2.9 %unpack.1 = (f32[1,1,4,2,128,128]{5,4,3,2,1,0:T(8,128)}, f32[1,1,4,2,128,128]{5,4,3,2,1,0:T(8,128)}) custom-call(f32[1560,128]{1,0:T(8,128)} %bitcast.4), custom_call_target="tpu_custom_call" | custom-call | tf_op jit(solution)/shard_map/unpack/pallas_call | solution.py:384

commit v4 on v3

--- a/solution.py
+++ b/solution.py
@@ -71,18 +71,11 @@
     return jnp.concatenate([high, low, high], axis=0)
 
 
-def sandwich(first, re, im, second):
-    both = dot(first, right_plain([split(re), split(im)]))
-    stacked = jnp.concatenate([both[:, :N], both[:, N:]], axis=0)
-    out = dot(lhs3([split(stacked)]), second)
-    return out[:N], out[N:]
-
-
 def main_kernel(
     ham_in, sig_in, coup_in, pat_in, shift, weight, back,
     ham, sig, coup, pat,
     gout, blocks, bonds, greens, send, recv, mixed,
-    swap_send, swap_recv, bond_send, bond_recv,
+    swap_send, swap_recv, bond_send, bond_recv, share_send, share_recv,
     fwd_send, fwd_recv, ret_send, ret_recv, in_sems,
     x_sem, z_sem, y_sem, core_sem,
 ):
@@ -125,12 +118,12 @@
     tell(barrier, y_line + x_line + z_near + other_core)
 
     loads = [
-        pltpu.make_async_copy(ham_in, ham, in_sems.at[0]),
-        pltpu.make_async_copy(sig_in.at[ls[2]], sig.at[ls[2]], in_sems.at[1]),
-        pltpu.make_async_copy(sig_in.at[ls[1]], sig.at[ls[1]], in_sems.at[2]),
-        pltpu.make_async_copy(sig_in.at[ls[3]], sig.at[ls[3]], in_sems.at[3]),
-        pltpu.make_async_copy(coup_in, coup, in_sems.at[4]),
-        pltpu.make_async_copy(pat_in, pat, in_sems.at[5]),
+        pltpu.make_async_copy(coup_in, coup, in_sems.at[0]),
+        pltpu.make_async_copy(pat_in, pat, in_sems.at[1]),
+        pltpu.make_async_copy(ham_in, ham, in_sems.at[2]),
+        pltpu.make_async_copy(sig_in.at[ls[2]], sig.at[ls[2]], in_sems.at[3]),
+        pltpu.make_async_copy(sig_in.at[ls[1]], sig.at[ls[1]], in_sems.at[4]),
+        pltpu.make_async_copy(sig_in.at[ls[3]], sig.at[ls[3]], in_sems.at[5]),
         pltpu.make_async_copy(sig_in.at[l], sig.at[l], in_sems.at[6]),
     ]
     for load in loads:
@@ -167,24 +160,39 @@
             device_id=device(i, group, k), device_id_type=MESH,
         )
 
+    half = pl.ds(pl.multiple_of(k * (N // 2), 8), N // 2)
+
     def bond_copy(i):
         return pltpu.make_async_remote_copy(
-            src_ref=bonds.at[l], dst_ref=bonds.at[l], send_sem=bond_send, recv_sem=bond_recv,
+            src_ref=bonds.at[l, half], dst_ref=bonds.at[l, half],
+            send_sem=bond_send, recv_sem=bond_recv,
             device_id=device(i, group, k), device_id_type=MESH,
         )
 
+    def bond_share(i):
+        return pltpu.make_async_remote_copy(
+            src_ref=bonds.at[i, half], dst_ref=bonds.at[i, half],
+            send_sem=share_send, recv_sem=share_recv,
+            device_id=device(l, group, 1 - k), device_id_type=MESH,
+        )
+
     def keep(where, i, block):
         where[i, 0], where[i, 1] = block
 
     loads[0].wait()
     loads[1].wait()
+    bonds[l] = coup[...] * pat[...].astype(F32)
+    loads[2].wait()
+    loads[3].wait()
     keep(gout, ls[2], inverse(ls[2]))
     pl.semaphore_wait(barrier, LAYERS + XS + 3)
     tell(z_sem, z_near)
+    for d in (2, 1, 3):
+        bond_copy(ls[d]).start()
     swap(ls[2]).start()
 
-    loads[2].wait()
-    loads[3].wait()
+    loads[4].wait()
+    loads[5].wait()
     one, two = inverse(ls[1]), inverse(ls[3])
     keep(gout, ls[1], one)
     keep(gout, ls[3], two)
@@ -193,46 +201,47 @@
     pl.semaphore_wait(z_sem, 4)
     tell(x_sem, x_line)
 
-    loads[4].wait()
-    loads[5].wait()
-    bonds[l] = coup[...] * pat[...].astype(F32)
-    for i in (2, 1, 3):
-        bond_copy(ls[i]).start()
     loads[6].wait()
     keep(blocks, l, inverse(l))
     pl.semaphore_wait(x_sem, XS - 1)
     tell(y_sem, y_line)
 
+    halves = bonds.at[pl.ds(0, LAYERS - 1), pl.ds(0, N // 2)]
+    pltpu.make_async_copy(halves, halves, bond_recv).wait()
+    for d in (2, 1, 3):
+        bond_share(ls[d]).start()
+    pltpu.make_async_copy(halves, halves, share_recv).wait()
     three = blocks.at[pl.ds(0, LAYERS - 1)]
     pltpu.make_async_copy(three, three, swap_recv).wait()
-    bthree = bonds.at[pl.ds(0, LAYERS - 1)]
-    pltpu.make_async_copy(bthree, bthree, bond_recv).wait()
-
     pl.semaphore_wait(y_sem, LAYERS - 1)
     tell(core_sem, other_core)
 
     g = [(blocks[i, 0], blocks[i, 1]) for i in range(LAYERS)]
-    gl3 = [left_c(*b) for b in g]
-    gr3 = [right_c(*b) for b in g]
-    b_l, b_r, bt_l, bt_r = {}, {}, {}, {}
+
+    def ends(i, first, second):
+        re, im = g[i]
+        stacked = split(jnp.concatenate([re, im], axis=0))
+        head = dot(lhs3([stacked]), right_plain([first]))
+        tail = dot(lhs3([second]), right_plain([split(re), split(im)]))
+        return left_c(head[:N], head[N:]), right_c(tail[:, :N], tail[:, N:])
+
+    down_ends, up_ends = {}, {}
     for i in range(1, LAYERS):
         b = bonds[i]
         bs, bts = split(b), split(b.T)
-        b_l[i], bt_l[i] = lhs3([bs]), lhs3([bts])
-        b_r[i], bt_r[i] = right_plain([bs]), right_plain([bts])
-
-    def dress(i, term):
-        tre, tim = cmul(gl3[i], right_c(*term))
-        sre, sim = cmul(left_c(tre, tim), gr3[i])
+        down_ends[i] = ends(i, bs, bts)
+        up_ends[i - 1] = ends(i - 1, bts, bs)
+
+    def dress(i, ends, inner):
+        sre, sim = cmul(left_c(*cmul(ends[0], right_c(*inner))), ends[1])
         return g[i][0] + sre, g[i][1] + sim
 
     down = {0: g[0]}
     up = {LAYERS - 1: g[LAYERS - 1]}
     for step in range(1, LAYERS):
-        i = step
-        down[i] = dress(i, sandwich(b_l[i], *down[i - 1], bt_r[i]))
+        down[step] = dress(step, down_ends[step], down[step - 1])
         j = LAYERS - 1 - step
-        up[j] = dress(j, sandwich(bt_l[j + 1], *up[j + 1], b_r[j + 1]))
+        up[j] = dress(j, up_ends[j], up[j + 1])
     for c in range(2):
         zero = jnp.zeros((N, N), F32)
         greens[0, c] = zero
@@ -321,7 +330,8 @@
     sent = back.at[pl.ds(0, PEERS - 1)]
     pltpu.make_async_copy(sent, sent, ret_send).wait()
     pltpu.make_async_copy(three, three, swap_send).wait()
-    pltpu.make_async_copy(bthree, bthree, bond_send).wait()
+    pltpu.make_async_copy(halves, halves, bond_send).wait()
+    pltpu.make_async_copy(halves, halves, share_send).wait()
     for i in range(LAYERS):
         part = send.at[i] if i else send.at[0, pl.ds(0, PEERS - 1)]
         pltpu.make_async_copy(part, part, fwd_send).wait()
@@ -349,14 +359,13 @@
 
 
 def shards(hamiltonian, sigma_prev, coupling, coupling_pattern, phonon_shift, phonon_weight):
-    vmem = pl.BlockSpec(memory_space=pltpu.VMEM)
     smem = pl.BlockSpec(memory_space=pltpu.SMEM)
     dma = pltpu.SemaphoreType.DMA
     back = pl.pallas_call(
         main_kernel,
         out_shape=jax.ShapeDtypeStruct((PEERS + 1, 24, N), F32),
         in_specs=[pl.BlockSpec(memory_space=pl.ANY)] * 4 + [smem] * 2,
-        out_specs=vmem,
+        out_specs=pl.BlockSpec(memory_space=pl.ANY),
         scratch_shapes=[
             pltpu.VMEM((2, N, N), F32),
             pltpu.VMEM((4, 2, N, N), F32),
@@ -370,7 +379,7 @@
             pltpu.VMEM((MOMS, ENERGIES, 4, N), F32),
             pltpu.VMEM((MOMS, 6 * ENERGIES + 8, N), F32),
         ]
-        + [dma] * 8
+        + [dma] * 10
         + [dma((7,))]
         + [pltpu.SemaphoreType.REGULAR] * 4,
         compiler_params=pltpu.CompilerParams(collective_id=0, has_side_effects=True),

time: 64.5 us -> 61 us (0.946)
  Pallas kernels: 63.8 us -> 60.2 us
    pallas_call x1, Pallas kernels: 60.8 us -> 57.3 us  [shards(): pl.pallas_call(main_kernel, out_shape=jax.ShapeDtypeStruct((PEERS + 1, 24...]
where the time goes in v4:
time: 61 us; the launch traced here: 60.8 us
  Pallas kernels  60.2 us (99%)
  between operations  0.64 us (1%)
    pallas_call x1, Pallas kernels, shards(): pl.pallas_call(main_kernel, out_shape=jax.ShapeDtypeStruct((PEERS + 1, 24...  57.3 us
    pallas_call x1, Pallas kernels, shards(): pl.pallas_call(unpack_kernel, grid=(4,), out_shape=(shape, shape), in_spe...  2.92 us

profile of v4, /device:TPU:1, one launch (start us, length us, event | category | flops | bytes accessed | tf_op | source)
XLA Modules:
  0.0 60.8 jit_solution(12879007866980988083)
XLA Ops:
  0.6 57.3 %selfenergy.1 = f32[65,24,128]{2,1,0:T(8,128)} custom-call(f32[2,128,128]{2,1,0:T(8,128)} %bitcast.6, f32[4,2,128,128]{3,2,1,0:T(8,128)} %bitcast.5, f32[128,128]{1,0:T(8,128)} %bitcast.7, s32[128,128]{1,0:T(8,128)} %pat_in.1, s32[4]{0:T(128)} %shift.1, f32[4]{0:T(128)} %weight.1), custom_call_target="tpu_custom_call" | custom-call | tf_op jit(solution)/shard_map/selfenergy/pallas_call | solution.py:364
  57.9 2.9 %unpack.1 = (f32[1,1,4,2,128,128]{5,4,3,2,1,0:T(8,128)}, f32[1,1,4,2,128,128]{5,4,3,2,1,0:T(8,128)}) custom-call(f32[1560,128]{1,0:T(8,128)} %bitcast.4), custom_call_target="tpu_custom_call" | custom-call | tf_op jit(solution)/shard_map/unpack/pallas_call | solution.py:393

commit v5 on v4

--- a/solution.py
+++ b/solution.py
@@ -72,9 +72,9 @@
 
 
 def main_kernel(
-    ham_in, sig_in, coup_in, pat_in, shift, weight, back,
+    ham_in, sig_in, coup_in, pat_in, shift, weight, back_p, back_q,
     ham, sig, coup, pat,
-    gout, blocks, bonds, greens, send, recv, mixed,
+    gout, blocks, bonds, greens, send, recv, mixed_p, mixed_q,
     swap_send, swap_recv, bond_send, bond_recv, share_send, share_recv,
     fwd_send, fwd_recv, ret_send, ret_recv, in_sems,
     x_sem, z_sem, y_sem, core_sem,
@@ -254,6 +254,25 @@
     upper = rows < cols
     slot = group * LAYERS + l
 
+    def exchange(part, t):
+        layer = ls[t]
+
+        def forward(to_group, to_mom):
+            pltpu.make_async_remote_copy(
+                src_ref=send.at[part, layer, to_group * MOMS + to_mom],
+                dst_ref=recv.at[part, k, slot],
+                send_sem=fwd_send.at[part], recv_sem=fwd_recv.at[part],
+                device_id=device(layer, to_group, to_mom), device_id_type=MESH,
+            ).start()
+
+        plane(forward)
+        if t:
+            forward(group, k)
+        else:
+            pltpu.make_async_copy(
+                send.at[part, layer, group * MOMS + k], recv.at[part, k, slot], fwd_recv.at[part]
+            ).start()
+
     pl.semaphore_wait(core_sem, 1)
     for t in (2, 1, 3, 0):
         layer = ls[t]
@@ -262,25 +281,12 @@
         tre, tim = yre.T, yim.T
         pmat = jnp.where(upper, yre - tre, yim + tim)
         qmat = jnp.where(upper, yim - tim, yre + tre)
-        send[layer, :, 0, :] = pmat[: N // 2]
-        send[layer, :, 1, :] = pmat[N // 2 :]
-        send[layer, :, 2, :] = qmat[: N // 2]
-        send[layer, :, 3, :] = qmat[N // 2 :]
-
-        def forward(to_group, to_mom, layer=layer):
-            pltpu.make_async_remote_copy(
-                src_ref=send.at[layer, to_group * MOMS + to_mom], dst_ref=recv.at[k, slot],
-                send_sem=fwd_send, recv_sem=fwd_recv,
-                device_id=device(layer, to_group, to_mom), device_id_type=MESH,
-            ).start()
-
-        plane(forward)
-        if t:
-            forward(group, k)
-        else:
-            pltpu.make_async_copy(
-                send.at[layer, group * MOMS + k], recv.at[k, slot], fwd_recv
-            ).start()
+        for part, mat in enumerate((pmat, qmat)):
+            for r in range(2):
+                send[part, layer, :, r, :] = mat[r * PEERS : (r + 1) * PEERS]
+        exchange(0, t)
+    for t in (2, 1, 3, 0):
+        exchange(1, t)
 
     dist = rows - cols
     own = jnp.zeros((N, N), F32)
@@ -297,58 +303,71 @@
     les_w = jnp.concatenate(
         [jnp.concatenate([fown, fother], axis=1), jnp.concatenate([fother, fown], axis=1)], axis=0
     )
-    ret_l, les_l = lhs3([split(ret_w)]), lhs3([split(les_w)])
-
-    pltpu.make_async_copy(recv, recv, fwd_recv).wait()
-    pieces = []
-    for r in range(4):
-        pieces.append(split(jnp.concatenate([recv[0, :, r, :], recv[1, :, r, :]], axis=0)))
-    ret = dot(ret_l, right_plain(pieces))
-    les = dot(les_l, right_plain(pieces[:2]))
-    for c in range(MOMS):
-        for r in range(6):
-            src = ret if r < 4 else les
-            lane = (r if r < 4 else r - 4) * N
-            mixed[c, pl.ds(r, N, stride=6), :] = src[c * N : (c + 1) * N, lane : lane + N]
+    ret_l = lhs3([split(ret_w)])
+    both_l = jnp.concatenate([ret_l, lhs3([split(les_w)])], axis=0)
 
     spot = group * MOMS + k
 
-    def returning(to_group, to_mom):
-        pltpu.make_async_remote_copy(
-            src_ref=mixed.at[to_mom, pl.ds(pl.multiple_of(to_group * 24, 8), 24), :],
-            dst_ref=back.at[spot], send_sem=ret_send, recv_sem=ret_recv,
-            device_id=device(l, to_group, to_mom), device_id_type=MESH,
-        ).start()
-
-    plane(returning)
-    pltpu.make_async_copy(
-        mixed.at[k, pl.ds(pl.multiple_of(group * 24, 8), 24), :], back.at[spot], ret_recv
-    ).start()
-
-    whole = back.at[pl.ds(0, PEERS)]
-    pltpu.make_async_copy(whole, whole, ret_recv).wait()
-    sent = back.at[pl.ds(0, PEERS - 1)]
-    pltpu.make_async_copy(sent, sent, ret_send).wait()
+    def mix(part, left, mixed, back, kinds):
+        arrived = recv.at[part]
+        pltpu.make_async_copy(arrived, arrived, fwd_recv.at[part]).wait()
+        pieces = [
+            split(jnp.concatenate([recv[part, 0, :, r, :], recv[part, 1, :, r, :]], axis=0))
+            for r in range(2)
+        ]
+        out = dot(left, right_plain(pieces))
+        each = 2 * kinds
+        for kind in range(kinds):
+            for c in range(MOMS):
+                top = (kind * MOMS + c) * N
+                for r in range(2):
+                    mixed[c, pl.ds(2 * kind + r, N, stride=each), :] = out[
+                        top : top + N, r * N : (r + 1) * N
+                    ]
+        size = each * LAYERS
+
+        def source(to_group, to_mom):
+            return mixed.at[to_mom, pl.ds(pl.multiple_of(to_group * size, 8), size), :]
+
+        def returning(to_group, to_mom):
+            pltpu.make_async_remote_copy(
+                src_ref=source(to_group, to_mom), dst_ref=back.at[spot],
+                send_sem=ret_send.at[part], recv_sem=ret_recv.at[part],
+                device_id=device(l, to_group, to_mom), device_id_type=MESH,
+            ).start()
+
+        plane(returning)
+        pltpu.make_async_copy(source(group, k), back.at[spot], ret_recv.at[part]).start()
+
+    mix(0, both_l, mixed_p, back_p, 2)
+    mix(1, ret_l, mixed_q, back_q, 1)
+
+    for part, back in enumerate((back_p, back_q)):
+        whole = back.at[pl.ds(0, PEERS)]
+        pltpu.make_async_copy(whole, whole, ret_recv.at[part]).wait()
+        sent = back.at[pl.ds(0, PEERS - 1)]
+        pltpu.make_async_copy(sent, sent, ret_send.at[part]).wait()
+        for i in range(LAYERS):
+            gone = send.at[part, i] if i else send.at[part, 0, pl.ds(0, PEERS - 1)]
+            pltpu.make_async_copy(gone, gone, fwd_send.at[part]).wait()
     pltpu.make_async_copy(three, three, swap_send).wait()
     pltpu.make_async_copy(halves, halves, bond_send).wait()
     pltpu.make_async_copy(halves, halves, share_send).wait()
-    for i in range(LAYERS):
-        part = send.at[i] if i else send.at[0, pl.ds(0, PEERS - 1)]
-        pltpu.make_async_copy(part, part, fwd_send).wait()
-
-
-def unpack_kernel(back, ret, les):
+
+
+def unpack_kernel(back_p, back_q, ret, les):
     e = pl.program_id(0)
     rows = lax.broadcasted_iota(jnp.int32, (N, N), 0)
     cols = lax.broadcasted_iota(jnp.int32, (N, N), 1)
     upper = rows < cols
 
-    def whole(r):
+    def whole(back, each, r):
         return jnp.concatenate(
-            [back[pl.ds(6 * e + r + h, PEERS, stride=24), :] for h in range(2)], axis=0
+            [back[pl.ds(each * e + r + h, PEERS, stride=LAYERS * each), :] for h in range(2)],
+            axis=0,
         )
 
-    pmat, qmat, lmat = whole(0), whole(2), whole(4)
+    pmat, lmat, qmat = whole(back_p, 4, 0), whole(back_p, 4, 2), whole(back_q, 2, 0)
     pt, qt, lt = pmat.T, qmat.T, lmat.T
     off = rows != cols
     zero = jnp.zeros((N, N), F32)
@@ -361,11 +380,14 @@
 def shards(hamiltonian, sigma_prev, coupling, coupling_pattern, phonon_shift, phonon_weight):
     smem = pl.BlockSpec(memory_space=pltpu.SMEM)
     dma = pltpu.SemaphoreType.DMA
-    back = pl.pallas_call(
+    back_p, back_q = pl.pallas_call(
         main_kernel,
-        out_shape=jax.ShapeDtypeStruct((PEERS + 1, 24, N), F32),
+        out_shape=(
+            jax.ShapeDtypeStruct((PEERS + 1, 16, N), F32),
+            jax.ShapeDtypeStruct((PEERS + 1, 8, N), F32),
+        ),
         in_specs=[pl.BlockSpec(memory_space=pl.ANY)] * 4 + [smem] * 2,
-        out_specs=pl.BlockSpec(memory_space=pl.ANY),
+        out_specs=(pl.BlockSpec(memory_space=pl.ANY),) * 2,
         scratch_shapes=[
             pltpu.VMEM((2, N, N), F32),
             pltpu.VMEM((4, 2, N, N), F32),
@@ -375,11 +397,13 @@
             pltpu.VMEM((LAYERS, 2, N, N), F32),
             pltpu.VMEM((LAYERS, N, N), F32),
             pltpu.VMEM((LAYERS + 2, 2, N, N), F32),
-            pltpu.VMEM((LAYERS, PEERS, 4, N), F32),
-            pltpu.VMEM((MOMS, ENERGIES, 4, N), F32),
-            pltpu.VMEM((MOMS, 6 * ENERGIES + 8, N), F32),
+            pltpu.VMEM((2, LAYERS, PEERS, 2, N), F32),
+            pltpu.VMEM((2, MOMS, ENERGIES, 2, N), F32),
+            pltpu.VMEM((MOMS, 4 * ENERGIES + 8, N), F32),
+            pltpu.VMEM((MOMS, 2 * ENERGIES + 8, N), F32),
         ]
-        + [dma] * 10
+        + [dma] * 6
+        + [dma((2,))] * 4
         + [dma((7,))]
         + [pltpu.SemaphoreType.REGULAR] * 4,
         compiler_params=pltpu.CompilerParams(collective_id=0, has_side_effects=True),
@@ -394,10 +418,13 @@
         unpack_kernel,
         grid=(4,),
         out_shape=(shape, shape),
-        in_specs=[pl.BlockSpec(((PEERS + 1) * 24, N), lambda e: (0, 0))],
+        in_specs=[
+            pl.BlockSpec(((PEERS + 1) * 16, N), lambda e: (0, 0)),
+            pl.BlockSpec(((PEERS + 1) * 8, N), lambda e: (0, 0)),
+        ],
         out_specs=(out_spec, out_spec),
         name="unpack",
-    )(back.reshape((PEERS + 1) * 24, N))
+    )(back_p.reshape((PEERS + 1) * 16, N), back_q.reshape((PEERS + 1) * 8, N))
 
 
 def solution(mesh):

time: 61 us -> 57.7 us (0.946)
  Pallas kernels: 60.2 us -> 56.9 us
    pallas_call x1, Pallas kernels: 57.3 us -> 54 us  [shards(): pl.pallas_call(main_kernel, out_shape=(jax.ShapeDtypeStruct((PEERS + 1, 1...]
where the time goes in v5:
time: 57.7 us; the launch traced here: 57.6 us
  Pallas kernels  56.9 us (99%)
  between operations  0.64 us (1%)
    pallas_call x1, Pallas kernels, shards(): pl.pallas_call(main_kernel, out_shape=(jax.ShapeDtypeStruct((PEERS + 1, 1...  54 us
    pallas_call x1, Pallas kernels, shards(): pl.pallas_call(unpack_kernel, grid=(4,), out_shape=(shape, shape), in_spe...  2.93 us

profile of v5, /device:TPU:1, one launch (start us, length us, event | category | flops | bytes accessed | tf_op | source)
XLA Modules:
  0.0 57.6 jit_solution(17351701620488102498)
XLA Ops:
  0.6 54.0 %selfenergy.1 = (f32[65,16,128]{2,1,0:T(8,128)}, f32[65,8,128]{2,1,0:T(8,128)}) custom-call(f32[2,128,128]{2,1,0:T(8,128)} %bitcast.8, f32[4,2,128,128]{3,2,1,0:T(8,128)} %bitcast.6, f32[128,128]{1,0:T(8,128)} %bitcast.9, s32[128,128]{1,0:T(8,128)} %pat_in.1, s32[4]{0:T(128)} %shift.1, f32[4]{0:T(128)} %weight.1), custom_call_target="tpu_custom_call" | custom-call | tf_op jit(solution)/shard_map/selfenergy/pallas_call | solution.py:383
  54.6 2.9 %unpack.1 = (f32[1,1,4,2,128,128]{5,4,3,2,1,0:T(8,128)}, f32[1,1,4,2,128,128]{5,4,3,2,1,0:T(8,128)}) custom-call(f32[1040,128]{1,0:T(8,128)} %bitcast.5, f32[520,128]{1,0:T(8,128)} %bitcast.7), custom_call_target="tpu_custom_call" | custom-call | tf_op jit(solution)/shard_map/unpack/pallas_call | solution.py:417

commit v6 on v5

--- a/solution.py
+++ b/solution.py
@@ -15,6 +15,7 @@
 MOMS = 2
 PEERS = GROUPS * MOMS
 PHONONS = 4
+PART = N // (MOMS * XS)
 ORDER = [(dx, dk) for dx in (2, 1, 3, 0) for dk in (1, 0)]
 F32 = jnp.float32
 BF16 = jnp.bfloat16
@@ -72,10 +73,10 @@
 
 
 def main_kernel(
-    ham_in, sig_in, coup_in, pat_in, shift, weight, back_p, back_q,
-    ham, sig, coup, pat,
+    ham_in, sig_in, coup_in, pat_in, shift_in, weight_in, back_p, back_q,
+    ham, sig, coup, pat, shift, weight,
     gout, blocks, bonds, greens, send, recv, mixed_p, mixed_q,
-    swap_send, swap_recv, bond_send, bond_recv, share_send, share_recv,
+    swap_send, swap_recv, bond_send, bond_recv,
     fwd_send, fwd_recv, ret_send, ret_recv, in_sems,
     x_sem, z_sem, y_sem, core_sem,
 ):
@@ -125,6 +126,8 @@
         pltpu.make_async_copy(sig_in.at[ls[1]], sig.at[ls[1]], in_sems.at[4]),
         pltpu.make_async_copy(sig_in.at[ls[3]], sig.at[ls[3]], in_sems.at[5]),
         pltpu.make_async_copy(sig_in.at[l], sig.at[l], in_sems.at[6]),
+        pltpu.make_async_copy(shift_in, shift, in_sems.at[7]),
+        pltpu.make_async_copy(weight_in, weight, in_sems.at[8]),
     ]
     for load in loads:
         load.start()
@@ -161,34 +164,41 @@
         )
 
     half = pl.ds(pl.multiple_of(k * (N // 2), 8), N // 2)
-
-    def bond_copy(i):
+    part = pl.ds(pl.multiple_of((k * XS + x) * PART, 8), PART)
+    far = pl.ds(1, LAYERS - 1)
+
+    def bond_copy(d):
         return pltpu.make_async_remote_copy(
-            src_ref=bonds.at[l, half], dst_ref=bonds.at[l, half],
-            send_sem=bond_send, recv_sem=bond_recv,
-            device_id=device(i, group, k), device_id_type=MESH,
+            src_ref=bonds.at[0, part], dst_ref=bonds.at[LAYERS - d, part],
+            send_sem=bond_send.at[0], recv_sem=bond_recv.at[0],
+            device_id=device(ls[d], group, k), device_id_type=MESH,
         )
 
-    def bond_share(i):
+    def bond_share(rows, stage, target):
         return pltpu.make_async_remote_copy(
-            src_ref=bonds.at[i, half], dst_ref=bonds.at[i, half],
-            send_sem=share_send, recv_sem=share_recv,
-            device_id=device(l, group, 1 - k), device_id_type=MESH,
+            src_ref=bonds.at[far, rows], dst_ref=bonds.at[far, rows],
+            send_sem=bond_send.at[stage], recv_sem=bond_recv.at[stage],
+            device_id=target, device_id_type=MESH,
         )
+
+    bond_parts = [bonds.at[far, pl.ds(0, rows)] for rows in (PART, (XS - 1) * PART, N // 2)]
+
+    def bond_wait(stage, semaphores):
+        pltpu.make_async_copy(bond_parts[stage], bond_parts[stage], semaphores.at[stage]).wait()
 
     def keep(where, i, block):
         where[i, 0], where[i, 1] = block
 
     loads[0].wait()
     loads[1].wait()
-    bonds[l] = coup[...] * pat[...].astype(F32)
+    bonds[0] = coup[...] * pat[...].astype(F32)
     loads[2].wait()
     loads[3].wait()
     keep(gout, ls[2], inverse(ls[2]))
     pl.semaphore_wait(barrier, LAYERS + XS + 3)
     tell(z_sem, z_near)
     for d in (2, 1, 3):
-        bond_copy(ls[d]).start()
+        bond_copy(d).start()
     swap(ls[2]).start()
 
     loads[4].wait()
@@ -198,21 +208,21 @@
     keep(gout, ls[3], two)
     swap(ls[1]).start()
     swap(ls[3]).start()
+    loads[6].wait()
+    keep(blocks, l, inverse(l))
+    bond_wait(0, bond_recv)
+    for target in x_line:
+        bond_share(part, 1, target).start()
     pl.semaphore_wait(z_sem, 4)
     tell(x_sem, x_line)
-
-    loads[6].wait()
-    keep(blocks, l, inverse(l))
     pl.semaphore_wait(x_sem, XS - 1)
     tell(y_sem, y_line)
-
-    halves = bonds.at[pl.ds(0, LAYERS - 1), pl.ds(0, N // 2)]
-    pltpu.make_async_copy(halves, halves, bond_recv).wait()
-    for d in (2, 1, 3):
-        bond_share(ls[d]).start()
-    pltpu.make_async_copy(halves, halves, share_recv).wait()
+    bond_wait(1, bond_recv)
+    bond_share(half, 2, other_core[0]).start()
+
     three = blocks.at[pl.ds(0, LAYERS - 1)]
     pltpu.make_async_copy(three, three, swap_recv).wait()
+    bond_wait(2, bond_recv)
     pl.semaphore_wait(y_sem, LAYERS - 1)
     tell(core_sem, other_core)
 
@@ -227,7 +237,7 @@
 
     down_ends, up_ends = {}, {}
     for i in range(1, LAYERS):
-        b = bonds[i]
+        b = bonds[wrap(i - l + LAYERS, LAYERS)]
         bs, bts = split(b), split(b.T)
         down_ends[i] = ends(i, bs, bts)
         up_ends[i - 1] = ends(i - 1, bts, bs)
@@ -288,6 +298,8 @@
     for t in (2, 1, 3, 0):
         exchange(1, t)
 
+    loads[7].wait()
+    loads[8].wait()
     dist = rows - cols
     own = jnp.zeros((N, N), F32)
     other = jnp.zeros((N, N), F32)
@@ -351,8 +363,8 @@
             gone = send.at[part, i] if i else send.at[part, 0, pl.ds(0, PEERS - 1)]
             pltpu.make_async_copy(gone, gone, fwd_send.at[part]).wait()
     pltpu.make_async_copy(three, three, swap_send).wait()
-    pltpu.make_async_copy(halves, halves, bond_send).wait()
-    pltpu.make_async_copy(halves, halves, share_send).wait()
+    for stage in range(3):
+        bond_wait(stage, bond_send)
 
 
 def unpack_kernel(back_p, back_q, ret, les):
@@ -378,21 +390,22 @@
 
 
 def shards(hamiltonian, sigma_prev, coupling, coupling_pattern, phonon_shift, phonon_weight):
-    smem = pl.BlockSpec(memory_space=pltpu.SMEM)
     dma = pltpu.SemaphoreType.DMA
     back_p, back_q = pl.pallas_call(
         main_kernel,
         out_shape=(
-            jax.ShapeDtypeStruct((PEERS + 1, 16, N), F32),
-            jax.ShapeDtypeStruct((PEERS + 1, 8, N), F32),
+            pltpu.VMEM((PEERS + 1, 16, N), F32),
+            pltpu.VMEM((PEERS + 1, 8, N), F32),
         ),
-        in_specs=[pl.BlockSpec(memory_space=pl.ANY)] * 4 + [smem] * 2,
-        out_specs=(pl.BlockSpec(memory_space=pl.ANY),) * 2,
+        in_specs=[pl.BlockSpec(memory_space=pl.ANY)] * 6,
+        out_specs=(pl.BlockSpec(memory_space=pltpu.VMEM),) * 2,
         scratch_shapes=[
             pltpu.VMEM((2, N, N), F32),
             pltpu.VMEM((4, 2, N, N), F32),
             pltpu.VMEM((N, N), F32),
             pltpu.VMEM((N, N), jnp.int32),
+            pltpu.SMEM((PHONONS,), jnp.int32),
+            pltpu.SMEM((PHONONS,), F32),
             pltpu.VMEM((LAYERS, 2, N, N), F32),
             pltpu.VMEM((LAYERS, 2, N, N), F32),
             pltpu.VMEM((LAYERS, N, N), F32),
@@ -402,9 +415,10 @@
             pltpu.VMEM((MOMS, 4 * ENERGIES + 8, N), F32),
             pltpu.VMEM((MOMS, 2 * ENERGIES + 8, N), F32),
         ]
-        + [dma] * 6
+        + [dma] * 2
+        + [dma((3,))] * 2
         + [dma((2,))] * 4
-        + [dma((7,))]
+        + [dma((9,))]
         + [pltpu.SemaphoreType.REGULAR] * 4,
         compiler_params=pltpu.CompilerParams(collective_id=0, has_side_effects=True),
         name="selfenergy",
@@ -419,12 +433,15 @@
         grid=(4,),
         out_shape=(shape, shape),
         in_specs=[
-            pl.BlockSpec(((PEERS + 1) * 16, N), lambda e: (0, 0)),
-            pl.BlockSpec(((PEERS + 1) * 8, N), lambda e: (0, 0)),
+            pl.BlockSpec(memory_space=pltpu.VMEM),
+            pl.BlockSpec(memory_space=pltpu.VMEM),
         ],
         out_specs=(out_spec, out_spec),
         name="unpack",
-    )(back_p.reshape((PEERS + 1) * 16, N), back_q.reshape((PEERS + 1) * 8, N))
+    )(*(
+        pltpu.with_memory_space_constraint(back, pltpu.VMEM)
+        for back in (back_p.reshape((PEERS + 1) * 16, N), back_q.reshape((PEERS + 1) * 8, N))
+    ))
 
 
 def solution(mesh):

time: 57.7 us -> 55.5 us (0.962)
  Pallas kernels: 56.9 us -> 54.7 us
    pallas_call x1, Pallas kernels: 2.93 us -> 1.81 us  [shards(): pl.pallas_call(unpack_kernel, grid=(4,), out_shape=(shape, shape), in_spe...]
    pallas_call x1, Pallas kernels: 54 us -> 52.9 us  [shards(): pl.pallas_call(main_kernel, out_shape=(pltpu.VMEM((PEERS + 1, 16, N), F32...]
where the time goes in v6:
time: 55.5 us; the launch traced here: 55.4 us
  Pallas kernels  54.7 us (99%)
  between operations  0.64 us (1%)
    pallas_call x1, Pallas kernels, shards(): pl.pallas_call(main_kernel, out_shape=(pltpu.VMEM((PEERS + 1, 16, N), F32...  52.9 us
    pallas_call x1, Pallas kernels, shards(): pl.pallas_call(unpack_kernel, grid=(4,), out_shape=(shape, shape), in_spe...  1.81 us

profile of v6, /device:TPU:1, one launch (start us, length us, event | category | flops | bytes accessed | tf_op | source)
XLA Modules:
  0.0 55.4 jit_solution(6405584418319228494)
XLA Ops:
  0.6 52.9 %selfenergy.1 = (f32[65,16,128]{2,1,0:T(8,128)S(1)}, f32[65,8,128]{2,1,0:T(8,128)S(1)}) custom-call(f32[2,128,128]{2,1,0:T(8,128)} %bitcast.8, f32[4,2,128,128]{3,2,1,0:T(8,128)} %bitcast.7, f32[128,128]{1,0:T(8,128)} %bitcast.9, s32[128,128]{1,0:T(8,128)} %pat_in.1, s32[4]{0:T(128)} %shift_in.1, f32[4]{0:T(128)} %weight_in.1), custom_call_target="tpu_custom_call" | custom-call | tf_op jit(solution)/shard_map/selfenergy/pallas_call | solution.py:394
  53.6 1.8 %unpack.1 = (f32[1,1,4,2,128,128]{5,4,3,2,1,0:T(8,128)}, f32[1,1,4,2,128,128]{5,4,3,2,1,0:T(8,128)}) custom-call(f32[1040,128]{1,0:T(8,128)S(1)} %bitcast.5, f32[520,128]{1,0:T(8,128)S(1)} %bitcast.6), custom_call_target="tpu_custom_call" | custom-call | tf_op jit(solution)/shard_map/unpack/pallas_call | solution.py:431

commit v7 on v6

--- a/solution.py
+++ b/solution.py
@@ -78,7 +78,7 @@
     gout, blocks, bonds, greens, send, recv, mixed_p, mixed_q,
     swap_send, swap_recv, bond_send, bond_recv,
     fwd_send, fwd_recv, ret_send, ret_recv, in_sems,
-    x_sem, z_sem, y_sem, core_sem,
+    z_sem, z_sem2, y_sem, turn_sem,
 ):
     l = lax.axis_index("len")
     group = lax.axis_index("energy")
@@ -112,11 +112,12 @@
             pl.semaphore_signal(semaphore, inc=1, device_id=target, device_id_type=MESH)
 
     x_line = [device(l, z * XS + xs[i], k) for i in range(1, XS)]
+    x_other = [device(l, z * XS + xs[i], 1 - k) for i in range(1, XS)]
     z_near = [device(l, wrap(z + i, ZS) * XS + x, k) for i in (1, 2, ZS - 2, ZS - 1)]
     y_line = [device(ls[i], group, k) for i in range(1, LAYERS)]
     other_core = [device(l, group, 1 - k)]
     barrier = pltpu.get_barrier_semaphore()
-    tell(barrier, y_line + x_line + z_near + other_core)
+    tell(barrier, y_line + x_line + x_other + z_near + other_core)
 
     loads = [
         pltpu.make_async_copy(coup_in, coup, in_sems.at[0]),
@@ -195,36 +196,54 @@
     loads[2].wait()
     loads[3].wait()
     keep(gout, ls[2], inverse(ls[2]))
-    pl.semaphore_wait(barrier, LAYERS + XS + 3)
+    pl.semaphore_wait(barrier, LAYERS + 2 * XS + 2)
     tell(z_sem, z_near)
     for d in (2, 1, 3):
         bond_copy(d).start()
-    swap(ls[2]).start()
+
+    @pl.when(k == 0)
+    def _():
+        swap(ls[2]).start()
 
     loads[4].wait()
     loads[5].wait()
     one, two = inverse(ls[1]), inverse(ls[3])
     keep(gout, ls[1], one)
     keep(gout, ls[3], two)
-    swap(ls[1]).start()
-    swap(ls[3]).start()
+
+    @pl.when(k == 0)
+    def _():
+        swap(ls[1]).start()
+        swap(ls[3]).start()
+
+    pl.semaphore_wait(z_sem, 4)
+    tell(z_sem2, z_near)
     loads[6].wait()
     keep(blocks, l, inverse(l))
+
+    three = blocks.at[pl.ds(0, LAYERS - 1)]
+
+    @pl.when(k == 0)
+    def _():
+        tell(turn_sem, other_core)
+
     bond_wait(0, bond_recv)
     for target in x_line:
         bond_share(part, 1, target).start()
-    pl.semaphore_wait(z_sem, 4)
-    tell(x_sem, x_line)
-    pl.semaphore_wait(x_sem, XS - 1)
+
+    @pl.when(k == 1)
+    def _():
+        pl.semaphore_wait(turn_sem, 1)
+        for d in (2, 1, 3):
+            swap(ls[d]).start()
+
+    pl.semaphore_wait(z_sem2, 4)
     tell(y_sem, y_line)
     bond_wait(1, bond_recv)
     bond_share(half, 2, other_core[0]).start()
 
-    three = blocks.at[pl.ds(0, LAYERS - 1)]
     pltpu.make_async_copy(three, three, swap_recv).wait()
     bond_wait(2, bond_recv)
-    pl.semaphore_wait(y_sem, LAYERS - 1)
-    tell(core_sem, other_core)
 
     g = [(blocks[i, 0], blocks[i, 1]) for i in range(LAYERS)]
 
@@ -283,7 +302,7 @@
                 send.at[part, layer, group * MOMS + k], recv.at[part, k, slot], fwd_recv.at[part]
             ).start()
 
-    pl.semaphore_wait(core_sem, 1)
+    pl.semaphore_wait(y_sem, LAYERS - 1)
     for t in (2, 1, 3, 0):
         layer = ls[t]
         yre = greens[layer + 1, 0] + 0.5 * (greens[layer, 0] + greens[layer + 2, 0])

time: 55.5 us -> 55.2 us (level)
  no operation moved by 1% of the time
where the time goes in v7:
time: 55.2 us; the launch traced here: 55.1 us
  Pallas kernels  54.5 us (99%)
  between operations  0.64 us (1%)
    pallas_call x1, Pallas kernels, shards(): pl.pallas_call(main_kernel, out_shape=(pltpu.VMEM((PEERS + 1, 16, N), F32...  52.7 us
    pallas_call x1, Pallas kernels, shards(): pl.pallas_call(unpack_kernel, grid=(4,), out_shape=(shape, shape), in_spe...  1.81 us

profile of v7, /device:TPU:1, one launch (start us, length us, event | category | flops | bytes accessed | tf_op | source)
XLA Modules:
  0.0 55.1 jit_solution(11976284474470847672)
XLA Ops:
  0.6 52.7 %selfenergy.1 = (f32[65,16,128]{2,1,0:T(8,128)S(1)}, f32[65,8,128]{2,1,0:T(8,128)S(1)}) custom-call(f32[2,128,128]{2,1,0:T(8,128)} %bitcast.8, f32[4,2,128,128]{3,2,1,0:T(8,128)} %bitcast.7, f32[128,128]{1,0:T(8,128)} %bitcast.9, s32[128,128]{1,0:T(8,128)} %pat_in.1, s32[4]{0:T(128)} %shift_in.1, f32[4]{0:T(128)} %weight_in.1), custom_call_target="tpu_custom_call" | custom-call | tf_op jit(solution)/shard_map/selfenergy/pallas_call | solution.py:413
  53.3 1.8 %unpack.1 = (f32[1,1,4,2,128,128]{5,4,3,2,1,0:T(8,128)}, f32[1,1,4,2,128,128]{5,4,3,2,1,0:T(8,128)}) custom-call(f32[1040,128]{1,0:T(8,128)S(1)} %bitcast.5, f32[520,128]{1,0:T(8,128)S(1)} %bitcast.6), custom_call_target="tpu_custom_call" | custom-call | tf_op jit(solution)/shard_map/unpack/pallas_call | solution.py:450

commit v8 on v7

--- a/solution.py
+++ b/solution.py
@@ -72,10 +72,17 @@
     return jnp.concatenate([high, low, high], axis=0)
 
 
+def gather(back, each, i, first):
+    return jnp.concatenate(
+        [back[pl.ds(each * i + first + h, PEERS, stride=LAYERS * each), :] for h in range(2)],
+        axis=0,
+    )
+
+
 def main_kernel(
-    ham_in, sig_in, coup_in, pat_in, shift_in, weight_in, back_p, back_q,
+    ham_in, sig_in, coup_in, pat_in, shift_in, weight_in, lesser, base, back_q,
     ham, sig, coup, pat, shift, weight,
-    gout, blocks, bonds, greens, send, recv, mixed_p, mixed_q,
+    gout, blocks, bonds, greens, send, recv, mixed_p, mixed_q, back_p,
     swap_send, swap_recv, bond_send, bond_recv,
     fwd_send, fwd_recv, ret_send, ret_recv, in_sems,
     z_sem, z_sem2, y_sem, turn_sem,
@@ -337,8 +344,6 @@
     ret_l = lhs3([split(ret_w)])
     both_l = jnp.concatenate([ret_l, lhs3([split(les_w)])], axis=0)
 
-    spot = group * MOMS + k
-
     def mix(part, left, mixed, back, kinds):
         arrived = recv.at[part]
         pltpu.make_async_copy(arrived, arrived, fwd_recv.at[part]).wait()
@@ -356,6 +361,7 @@
                         top : top + N, r * N : (r + 1) * N
                     ]
         size = each * LAYERS
+        spot = pl.ds(pl.multiple_of((group * MOMS + k) * size, 8), size)
 
         def source(to_group, to_mom):
             return mixed.at[to_mom, pl.ds(pl.multiple_of(to_group * size, 8), size), :]
@@ -373,10 +379,24 @@
     mix(0, both_l, mixed_p, back_p, 2)
     mix(1, ret_l, mixed_q, back_q, 1)
 
-    for part, back in enumerate((back_p, back_q)):
-        whole = back.at[pl.ds(0, PEERS)]
+    def arrive(part, back, size):
+        whole = back.at[pl.ds(0, PEERS * size)]
         pltpu.make_async_copy(whole, whole, ret_recv.at[part]).wait()
-        sent = back.at[pl.ds(0, PEERS - 1)]
+
+    arrive(0, back_p, 16)
+    off = rows != cols
+    zero = jnp.zeros((N, N), F32)
+    for i in range(LAYERS):
+        pmat, lmat = gather(back_p, 4, i, 0), gather(back_p, 4, i, 2)
+        pt, lt = pmat.T, lmat.T
+        lesser[i, 0] = jnp.where(upper, lmat, jnp.where(off, -lt, zero))
+        lesser[i, 1] = jnp.where(upper, lt, lmat)
+        base[i, 0] = 0.5 * jnp.where(upper, pmat, jnp.where(off, -pt, zero))
+        base[i, 1] = 0.5 * jnp.where(upper, pt, pmat)
+    arrive(1, back_q, 8)
+
+    for part, (back, size) in enumerate(((back_p, 16), (back_q, 8))):
+        sent = back.at[pl.ds(0, (PEERS - 1) * size)]
         pltpu.make_async_copy(sent, sent, ret_send.at[part]).wait()
         for i in range(LAYERS):
             gone = send.at[part, i] if i else send.at[part, 0, pl.ds(0, PEERS - 1)]
@@ -386,38 +406,39 @@
         bond_wait(stage, bond_send)
 
 
-def unpack_kernel(back_p, back_q, ret, les):
-    e = pl.program_id(0)
+def unpack_kernel(lesser, base, back_q, ret, les, out, sems):
+    lesser_copy = pltpu.make_async_copy(lesser, les.at[0, 0], sems.at[LAYERS])
+    lesser_copy.start()
     rows = lax.broadcasted_iota(jnp.int32, (N, N), 0)
     cols = lax.broadcasted_iota(jnp.int32, (N, N), 1)
     upper = rows < cols
-
-    def whole(back, each, r):
-        return jnp.concatenate(
-            [back[pl.ds(each * e + r + h, PEERS, stride=LAYERS * each), :] for h in range(2)],
-            axis=0,
-        )
-
-    pmat, lmat, qmat = whole(back_p, 4, 0), whole(back_p, 4, 2), whole(back_q, 2, 0)
-    pt, qt, lt = pmat.T, qmat.T, lmat.T
     off = rows != cols
     zero = jnp.zeros((N, N), F32)
-    ret[0, 0, 0, 0] = 0.5 * jnp.where(upper, pmat + qt, qmat - jnp.where(off, pt, zero))
-    ret[0, 0, 0, 1] = 0.5 * jnp.where(upper, pt + qmat, pmat - jnp.where(off, qt, zero))
-    les[0, 0, 0, 0] = jnp.where(upper, lmat, jnp.where(off, -lt, zero))
-    les[0, 0, 0, 1] = jnp.where(upper, lt, lmat)
+    copies = [
+        pltpu.make_async_copy(out.at[i], ret.at[0, 0, i], sems.at[i]) for i in range(LAYERS)
+    ]
+    for i in range(LAYERS):
+        qmat = gather(back_q, 2, i, 0)
+        qt = qmat.T
+        out[i, 0] = base[i, 0] + 0.5 * jnp.where(upper, qt, qmat)
+        out[i, 1] = base[i, 1] + 0.5 * jnp.where(upper, qmat, jnp.where(off, -qt, zero))
+        copies[i].start()
+    for copy in copies:
+        copy.wait()
+    lesser_copy.wait()
 
 
 def shards(hamiltonian, sigma_prev, coupling, coupling_pattern, phonon_shift, phonon_weight):
     dma = pltpu.SemaphoreType.DMA
-    back_p, back_q = pl.pallas_call(
+    found = pl.pallas_call(
         main_kernel,
         out_shape=(
-            pltpu.VMEM((PEERS + 1, 16, N), F32),
-            pltpu.VMEM((PEERS + 1, 8, N), F32),
+            pltpu.VMEM((LAYERS, 2, N, N), F32),
+            pltpu.VMEM((LAYERS, 2, N, N), F32),
+            pltpu.VMEM(((PEERS + 1) * 8, N), F32),
         ),
         in_specs=[pl.BlockSpec(memory_space=pl.ANY)] * 6,
-        out_specs=(pl.BlockSpec(memory_space=pltpu.VMEM),) * 2,
+        out_specs=(pl.BlockSpec(memory_space=pltpu.VMEM),) * 3,
         scratch_shapes=[
             pltpu.VMEM((2, N, N), F32),
             pltpu.VMEM((4, 2, N, N), F32),
@@ -433,6 +454,7 @@
             pltpu.VMEM((2, MOMS, ENERGIES, 2, N), F32),
             pltpu.VMEM((MOMS, 4 * ENERGIES + 8, N), F32),
             pltpu.VMEM((MOMS, 2 * ENERGIES + 8, N), F32),
+            pltpu.VMEM(((PEERS + 1) * 16, N), F32),
         ]
         + [dma] * 2
         + [dma((3,))] * 2
@@ -446,21 +468,14 @@
         phonon_shift, phonon_weight,
     )
     shape = jax.ShapeDtypeStruct((1, 1, 4, 2, N, N), F32)
-    out_spec = pl.BlockSpec((1, 1, 1, 2, N, N), lambda e: (0, 0, e, 0, 0, 0))
     return pl.pallas_call(
         unpack_kernel,
-        grid=(4,),
         out_shape=(shape, shape),
-        in_specs=[
-            pl.BlockSpec(memory_space=pltpu.VMEM),
-            pl.BlockSpec(memory_space=pltpu.VMEM),
-        ],
-        out_specs=(out_spec, out_spec),
+        in_specs=[pl.BlockSpec(memory_space=pltpu.VMEM)] * 3,
+        out_specs=(pl.BlockSpec(memory_space=pl.ANY),) * 2,
+        scratch_shapes=[pltpu.VMEM((LAYERS, 2, N, N), F32), dma((LAYERS + 1,))],
         name="unpack",
-    )(*(
-        pltpu.with_memory_space_constraint(back, pltpu.VMEM)
-        for back in (back_p.reshape((PEERS + 1) * 16, N), back_q.reshape((PEERS + 1) * 8, N))
-    ))
+    )(*(pltpu.with_memory_space_constraint(value, pltpu.VMEM) for value in found))
 
 
 def solution(mesh):

time: 55.2 us -> 54.4 us (0.986)
  Pallas kernels: 54.5 us -> 53.7 us
    pallas_call x2, Pallas kernels: 54.5 us -> 53.7 us  [the longest x1 52.7 us: shards(): pl.pallas_call(main_kernel, out_shape=(pltpu.VMEM((LAYERS, 2, N, N), F32)...]
where the time goes in v8:
time: 54.4 us; the launch traced here: 54.3 us
  Pallas kernels  53.7 us (99%)
  between operations  0.64 us (1%)
    pallas_call x1, Pallas kernels, shards(): pl.pallas_call(main_kernel, out_shape=(pltpu.VMEM((LAYERS, 2, N, N), F32)...  52.7 us

profile of v8, /device:TPU:1, one launch (start us, length us, event | category | flops | bytes accessed | tf_op | source)
XLA Modules:
  0.0 54.3 jit_solution(16168486538918520152)
XLA Ops:
  0.6 52.7 %selfenergy.1 = (f32[4,2,128,128]{3,2,1,0:T(8,128)S(1)}, f32[4,2,128,128]{3,2,1,0:T(8,128)S(1)}, f32[520,128]{1,0:T(8,128)S(1)}) custom-call(f32[2,128,128]{2,1,0:T(8,128)} %bitcast.4, f32[4,2,128,128]{3,2,1,0:T(8,128)} %bitcast.3, f32[128,128]{1,0:T(8,128)} %bitcast.5, s32[128,128]{1,0:T(8,128)} %pat_in.1, s32[4]{0:T(128)} %shift_in.1, f32[4]{0:T(128)} %weight_in.1), custom_call_target="tpu_custom_call" | custom-call | tf_op jit(solution)/shard_map/selfenergy/pallas_call | solution.py:433
  53.3 1.0 %unpack.1 = (f32[1,1,4,2,128,128]{5,4,3,2,1,0:T(8,128)}, f32[1,1,4,2,128,128]{5,4,3,2,1,0:T(8,128)}) custom-call(f32[4,2,128,128]{3,2,1,0:T(8,128)S(1)} %get-tuple-element.5.lesser, f32[4,2,128,128]{3,2,1,0:T(8,128)S(1)} %get-tuple-element.6.base, f32[520,128]{1,0:T(8,128)S(1)} %get-tuple-element.7.back_q), custom_call_target="tpu_custom_call" | custom-call | tf_op jit(solution)/shard_map/unpack/pallas_call | solution.py:471

commit v9 on v8

--- a/solution.py
+++ b/solution.py
@@ -232,6 +232,7 @@
 
     @pl.when(k == 0)
     def _():
+        pltpu.make_async_copy(three, three, swap_send).wait()
         tell(turn_sem, other_core)
 
     bond_wait(0, bond_recv)
@@ -401,7 +402,10 @@
         for i in range(LAYERS):
             gone = send.at[part, i] if i else send.at[part, 0, pl.ds(0, PEERS - 1)]
             pltpu.make_async_copy(gone, gone, fwd_send.at[part]).wait()
-    pltpu.make_async_copy(three, three, swap_send).wait()
+    @pl.when(k == 1)
+    def _():
+        pltpu.make_async_copy(three, three, swap_send).wait()
+
     for stage in range(3):
         bond_wait(stage, bond_send)
 

time: 54.4 us -> 54.2 us (level)
  no operation moved by 1% of the time
where the time goes in v9:
time: 54.2 us; the launch traced here: 54.1 us
  Pallas kernels  53.4 us (99%)
  between operations  0.64 us (1%)
    pallas_call x1, Pallas kernels, shards(): pl.pallas_call(main_kernel, out_shape=(pltpu.VMEM((LAYERS, 2, N, N), F32)...  52.4 us

profile of v9, /device:TPU:1, one launch (start us, length us, event | category | flops | bytes accessed | tf_op | source)
XLA Modules:
  0.0 54.1 jit_solution(12308170755453988692)
XLA Ops:
  0.6 52.4 %selfenergy.1 = (f32[4,2,128,128]{3,2,1,0:T(8,128)S(1)}, f32[4,2,128,128]{3,2,1,0:T(8,128)S(1)}, f32[520,128]{1,0:T(8,128)S(1)}) custom-call(f32[2,128,128]{2,1,0:T(8,128)} %bitcast.4, f32[4,2,128,128]{3,2,1,0:T(8,128)} %bitcast.3, f32[128,128]{1,0:T(8,128)} %bitcast.5, s32[128,128]{1,0:T(8,128)} %pat_in.1, s32[4]{0:T(128)} %shift_in.1, f32[4]{0:T(128)} %weight_in.1), custom_call_target="tpu_custom_call" | custom-call | tf_op jit(solution)/shard_map/selfenergy/pallas_call | solution.py:437
  53.0 1.0 %unpack.1 = (f32[1,1,4,2,128,128]{5,4,3,2,1,0:T(8,128)}, f32[1,1,4,2,128,128]{5,4,3,2,1,0:T(8,128)}) custom-call(f32[4,2,128,128]{3,2,1,0:T(8,128)S(1)} %get-tuple-element.5.lesser, f32[4,2,128,128]{3,2,1,0:T(8,128)S(1)} %get-tuple-element.6.base, f32[520,128]{1,0:T(8,128)S(1)} %get-tuple-element.7.back_q), custom_call_target="tpu_custom_call" | custom-call | tf_op jit(solution)/shard_map/unpack/pallas_call | solution.py:475

commit v10 on v9

--- a/solution.py
+++ b/solution.py
@@ -230,14 +230,14 @@
 
     three = blocks.at[pl.ds(0, LAYERS - 1)]
 
+    bond_wait(0, bond_recv)
+    for target in x_line:
+        bond_share(part, 1, target).start()
+
     @pl.when(k == 0)
     def _():
         pltpu.make_async_copy(three, three, swap_send).wait()
         tell(turn_sem, other_core)
-
-    bond_wait(0, bond_recv)
-    for target in x_line:
-        bond_share(part, 1, target).start()
 
     @pl.when(k == 1)
     def _():

time: 54.2 us -> 54.3 us (level)
  no operation moved by 1% of the time
where the time goes in v10:
time: 54.3 us; the launch traced here: 54.2 us
  Pallas kernels  53.6 us (99%)
  between operations  0.64 us (1%)
    pallas_call x1, Pallas kernels, shards(): pl.pallas_call(main_kernel, out_shape=(pltpu.VMEM((LAYERS, 2, N, N), F32)...  52.6 us

profile of v10, /device:TPU:1, one launch (start us, length us, event | category | flops | bytes accessed | tf_op | source)
XLA Modules:
  0.0 54.2 jit_solution(12919355728338064145)
XLA Ops:
  0.6 52.6 %selfenergy.1 = (f32[4,2,128,128]{3,2,1,0:T(8,128)S(1)}, f32[4,2,128,128]{3,2,1,0:T(8,128)S(1)}, f32[520,128]{1,0:T(8,128)S(1)}) custom-call(f32[2,128,128]{2,1,0:T(8,128)} %bitcast.4, f32[4,2,128,128]{3,2,1,0:T(8,128)} %bitcast.3, f32[128,128]{1,0:T(8,128)} %bitcast.5, s32[128,128]{1,0:T(8,128)} %pat_in.1, s32[4]{0:T(128)} %shift_in.1, f32[4]{0:T(128)} %weight_in.1), custom_call_target="tpu_custom_call" | custom-call | tf_op jit(solution)/shard_map/selfenergy/pallas_call | solution.py:437
  53.2 1.0 %unpack.1 = (f32[1,1,4,2,128,128]{5,4,3,2,1,0:T(8,128)}, f32[1,1,4,2,128,128]{5,4,3,2,1,0:T(8,128)}) custom-call(f32[4,2,128,128]{3,2,1,0:T(8,128)S(1)} %get-tuple-element.5.lesser, f32[4,2,128,128]{3,2,1,0:T(8,128)S(1)} %get-tuple-element.6.base, f32[520,128]{1,0:T(8,128)S(1)} %get-tuple-element.7.back_q), custom_call_target="tpu_custom_call" | custom-call | tf_op jit(solution)/shard_map/unpack/pallas_call | solution.py:475
